TPU v7x, 32 devices: a whole 2x2x4 slice. The times are simulated.
32 devices in a mesh: dp: 2 (over x), row: 4 (over z), col: 4 (over y, core).
Axes of the slice: x: 2, y: 2, z: 4, core: 2. Of those that a mesh axis runs over, the one named last changes fastest.
Arguments:
- hidden_in: bfloat16 [4096, 1024], P(('dp', 'row'), 'col'), may hold values from -18 to 18
- doc_ids: int32 [8, 512], P(('dp', 'row')), may hold values from 0 to 3, as said below
- w_qkv: bfloat16 [1024, 3, 1024], P('row', None, 'col'), may hold values from -0.1875 to 0.1875
- query_bias: float32 [1024], P('col'), may hold values from -3 to 3
- value_bias: float32 [1024], P('col'), may hold values from -3 to 3
- w_out: bfloat16 [1024, 1024], P('col', 'row'), may hold values from -0.75 to 0.75
- out_bias: float32 [1024], P('col'), may hold values from -3 to 3
- norm_gain: float32 [1024], P('col'), may hold values from 0.5 to 1.5
- norm_shift: float32 [1024], P('col'), may hold values from -3 to 3
- w_up: bfloat16 [1024, 4096], P('row', 'col'), may hold values from -0.1875 to 0.1875
- up_bias: float32 [4096], P('col'), may hold values from -3 to 3
- w_down: bfloat16 [4096, 1024], P('col', 'row'), may hold values from -0.09375 to 0.09375
- down_bias: float32 [1024], P('col'), may hold values from -3 to 3
- final_gain: float32 [1024], P('col'), may hold values from 0.5 to 1.5
- final_shift: float32 [1024], P('col'), may hold values from -3 to 3
- out_grad: bfloat16 [4096, 1024], P(('dp', 'row'), 'col'), may hold values from -6 to 6
Outputs:
- layer_out: bfloat16 [4096, 1024], P(('dp', 'row'), 'col')
- hidden_grad: float32 [4096, 1024], P(('dp', 'row'), 'col')
- wqkv_grad: float32 [1024, 3, 1024], P('row', None, 'col')
- qbias_grad: float32 [1024], P('col')
- vbias_grad: float32 [1024], P('col')
- wout_grad: float32 [1024, 1024], P('col', 'row')
- obias_grad: float32 [1024], P('col')
- ngain_grad: float32 [1024], P('col')
- nshift_grad: float32 [1024], P('col')
- wup_grad: float32 [1024, 4096], P('row', 'col')
- ubias_grad: float32 [4096], P('col')
- wdown_grad: float32 [4096, 1024], P('col', 'row')
- dbias_grad: float32 [1024], P('col')
- fgain_grad: float32 [1024], P('col')
- fshift_grad: float32 [1024], P('col')
Inputs may be any that keep to these rules, and one draw needn't show every extreme that they name: `doc_ids`: along each sequence the ids never fall, start at 0 and end at 3: every sequence packs four documents, each of 51 tokens or more.
All inputs are finite; a program needn't handle non-finite values.
Results may differ from a plain program's by a relative error of at most 0.015.
Values may be sent and summed in bfloat16 or wider, within the bound.
A program may use at most 128 MiB of HBM per device.

v0:
```python
import jax
import jax.numpy as jnp
from jax import lax
from jax.sharding import PartitionSpec as P

D = 1024
HD = 64


EPS = 1e-12
INV_ROOT_TWO = 0.7071067811865476
INV_ROOT_PI = 0.3989422804014327


def gelu_parts(pre_act):
    cdf_val = 0.5 * (1.0 + lax.erf(pre_act * INV_ROOT_TWO))
    density = jnp.exp(-0.5 * pre_act * pre_act) * INV_ROOT_PI
    return (pre_act * cdf_val, cdf_val + pre_act * density)


def normalize(total, gain, shift):
    mean_val = lax.psum(jnp.sum(total, axis=1), "col") / D
    centered = total - mean_val[:, None]
    variance = lax.psum(jnp.sum(centered * centered, axis=1), "col") / D
    inverse = lax.rsqrt(variance + EPS)[:, None]
    normed = centered * inverse
    return (normed * gain + shift, normed, inverse)


def norm_back(upstream, normed, inverse, gain):
    scaled = upstream * gain
    first_sum, second = lax.psum((jnp.sum(scaled, axis=1), jnp.sum(scaled * normed, axis=1)), "col")
    return inverse * (scaled - first_sum[:, None] / D - normed * (second[:, None] / D))


def spread(block):
    return lax.all_gather(block, "col", axis=1, tiled=True)


def spread_grad(block):
    return lax.all_gather(block, "col", axis=1, tiled=True)


def collect(partial_sum):
    return lax.psum_scatter(partial_sum, "col", scatter_dimension=1, tiled=True)


def collect_back(partial_sum):
    return lax.psum_scatter(partial_sum, "col", scatter_dimension=1, tiled=True)


def seq_scores(query, keys, doc_row):
    same_doc = doc_row[:, None] == doc_row[None, :]
    scores = jnp.einsum("qhd,khd->hqk", query, keys, preferred_element_type=jnp.float32) * HD ** (
        -0.5
    )
    return jnp.where(same_doc[None], scores, -jnp.inf)


def attend_seq(inputs_seq):
    query, keys, values, doc_row = inputs_seq
    scores = seq_scores(query, keys, doc_row)
    top_score = jnp.max(scores, axis=-1, keepdims=True)
    log_total = top_score + jnp.log(jnp.sum(jnp.exp(scores - top_score), axis=-1, keepdims=True))
    prob_bf = jnp.exp(scores - log_total).astype(jnp.bfloat16)
    context = jnp.einsum(
        "hqk,khd->qhd", prob_bf, values, preferred_element_type=jnp.float32
    ).astype(jnp.bfloat16)
    return (context, log_total)


def attend_back(inputs_seq):
    query, keys, values, doc_row, ctx_back, log_total = inputs_seq
    prob_f = jnp.exp(seq_scores(query, keys, doc_row) - log_total)
    v_back = jnp.einsum(
        "hqk,qhd->khd", prob_f.astype(jnp.bfloat16), ctx_back, preferred_element_type=jnp.float32
    )
    d_prob = jnp.einsum("qhd,khd->hqk", ctx_back, values, preferred_element_type=jnp.float32)
    row_delta = jnp.sum(prob_f * d_prob, axis=-1, keepdims=True)
    score_back = (prob_f * (d_prob - row_delta) * HD ** (-0.5)).astype(jnp.bfloat16)
    q_back = jnp.einsum("hqk,khd->qhd", score_back, keys, preferred_element_type=jnp.float32)
    k_back = jnp.einsum("hqk,qhd->khd", score_back, query, preferred_element_type=jnp.float32)
    return (q_back, k_back, v_back)


def per_device(
    hidden_in,
    doc_ids,
    w_qkv,
    query_bias,
    value_bias,
    w_out,
    out_bias,
    norm_gain,
    norm_shift,
    w_up,
    up_bias,
    w_down,
    down_bias,
    final_gain,
    final_shift,
    out_grad,
):
    f32 = jnp.float32
    bf16 = jnp.bfloat16
    qkv_full, out_full, up_full, down_full = (
        lax.all_gather(w_qkv, "row", axis=0, tiled=True),
        lax.all_gather(w_out, "row", axis=1, tiled=True),
        lax.all_gather(w_up, "row", axis=0, tiled=True),
        lax.all_gather(w_down, "row", axis=1, tiled=True),
    )
    tokens_dev = hidden_in.shape[0]
    col_width = hidden_in.shape[1]
    head_count = col_width // HD
    seq_count = doc_ids.shape[0]
    seq_len = doc_ids.shape[1]
    head_shape = (seq_count, seq_len, head_count, HD)
    x_full = spread(hidden_in)
    projected = jnp.einsum("td,dkc->tkc", x_full, qkv_full, preferred_element_type=f32)
    query = (projected[:, 0] + query_bias).astype(bf16).reshape(head_shape)
    keys = projected[:, 1].astype(bf16).reshape(head_shape)
    values = (projected[:, 2] + value_bias).astype(bf16).reshape(head_shape)
    context, log_total = lax.map(attend_seq, (query, keys, values, doc_ids))
    ctx_rows = context.reshape(tokens_dev, col_width)
    total_one = (
        hidden_in.astype(f32)
        + collect(jnp.dot(ctx_rows, out_full, preferred_element_type=f32))
        + out_bias
    )
    attn_act, normed_one, inverse_one = normalize(total_one, norm_gain, norm_shift)
    attn_bf = attn_act.astype(bf16)
    attn_full = spread(attn_bf)
    up_pre = jnp.dot(attn_full, up_full, preferred_element_type=f32) + up_bias
    act_f, slope = gelu_parts(up_pre)
    act = act_f.astype(bf16)
    total_two = attn_act + collect(jnp.dot(act, down_full, preferred_element_type=f32)) + down_bias
    final, normed_two, inverse_two = normalize(total_two, final_gain, final_shift)
    layer_out = final.astype(bf16)
    grad_top = out_grad.astype(f32)
    fgain_part = jnp.sum(grad_top * normed_two, axis=0)
    fshift_part = jnp.sum(grad_top, axis=0)
    back_two = norm_back(grad_top, normed_two, inverse_two, final_gain)
    back_two_full = spread_grad(back_two.astype(bf16))
    wdown_part = jnp.dot(act.T, back_two_full, preferred_element_type=f32)
    dbias_part = jnp.sum(back_two, axis=0)
    up_back = jnp.dot(back_two_full, down_full.T, preferred_element_type=f32) * slope
    up_back_bf = up_back.astype(bf16)
    wup_part = jnp.dot(attn_full.T, up_back_bf, preferred_element_type=f32)
    ubias_part = jnp.sum(up_back, axis=0)
    attn_back = back_two + collect_back(jnp.dot(up_back_bf, up_full.T, preferred_element_type=f32))
    ngain_part = jnp.sum(attn_back * normed_one, axis=0)
    nshift_part = jnp.sum(attn_back, axis=0)
    back_one = norm_back(attn_back, normed_one, inverse_one, norm_gain)
    back_one_full = spread_grad(back_one.astype(bf16))
    wout_part = jnp.dot(ctx_rows.T, back_one_full, preferred_element_type=f32)
    obias_part = jnp.sum(back_one, axis=0)
    ctx_back = (
        jnp.dot(back_one_full, out_full.T, preferred_element_type=f32)
        .astype(bf16)
        .reshape(head_shape)
    )
    q_back, k_back, v_back = lax.map(
        attend_back, (query, keys, values, doc_ids, ctx_back, log_total)
    )
    q_back = q_back.reshape(tokens_dev, col_width)
    k_back = k_back.reshape(tokens_dev, col_width)
    v_back = v_back.reshape(tokens_dev, col_width)
    qbias_part = jnp.sum(q_back, axis=0)
    vbias_part = jnp.sum(v_back, axis=0)
    qkv_back = jnp.stack([q_back, k_back, v_back], axis=1).astype(bf16)
    wqkv_part = jnp.einsum("td,tkc->dkc", x_full, qkv_back, preferred_element_type=f32)
    hidden_grad = back_one + collect_back(
        jnp.einsum("tkc,dkc->td", qkv_back, qkv_full, preferred_element_type=f32)
    )
    pieces = (
        lax.psum_scatter(
            wqkv_part.astype(jnp.bfloat16), "row", scatter_dimension=0, tiled=True
        ).astype(jnp.float32),
        lax.psum_scatter(
            wout_part.astype(jnp.bfloat16), "row", scatter_dimension=1, tiled=True
        ).astype(jnp.float32),
        lax.psum_scatter(
            wup_part.astype(jnp.bfloat16), "row", scatter_dimension=0, tiled=True
        ).astype(jnp.float32),
        lax.psum_scatter(
            wdown_part.astype(jnp.bfloat16), "row", scatter_dimension=1, tiled=True
        ).astype(jnp.float32),
    )
    wqkv_grad, wout_grad, wup_grad, wdown_grad = (
        lax.psum(pieces[0].astype(jnp.bfloat16), "dp").astype(jnp.float32),
        lax.psum(pieces[1].astype(jnp.bfloat16), "dp").astype(jnp.float32),
        lax.psum(pieces[2].astype(jnp.bfloat16), "dp").astype(jnp.float32),
        lax.psum(pieces[3].astype(jnp.bfloat16), "dp").astype(jnp.float32),
    )
    small_sums = lax.psum(
        (
            qbias_part,
            vbias_part,
            obias_part,
            ngain_part,
            nshift_part,
            ubias_part,
            dbias_part,
            fgain_part,
            fshift_part,
        ),
        ("dp", "row"),
    )
    return (
        layer_out,
        hidden_grad,
        wqkv_grad,
        small_sums[0],
        small_sums[1],
        wout_grad,
        small_sums[2],
        small_sums[3],
        small_sums[4],
        wup_grad,
        small_sums[5],
        wdown_grad,
        small_sums[6],
        small_sums[7],
        small_sums[8],
    )


def solution(mesh):
    placed = (
        P(("dp", "row"), "col"),
        P(("dp", "row"), None),
        P("row", None, "col"),
        P("col"),
        P("col"),
        P("col", "row"),
        P("col"),
        P("col"),
        P("col"),
        P("row", "col"),
        P("col"),
        P("col", "row"),
        P("col"),
        P("col"),
        P("col"),
        P(("dp", "row"), "col"),
    )
    return jax.shard_map(
        per_device,
        mesh=mesh,
        in_specs=placed,
        out_specs=(
            P(("dp", "row"), "col"),
            P(("dp", "row"), "col"),
            P("row", None, "col"),
            P("col"),
            P("col"),
            P("col", "row"),
            P("col"),
            P("col"),
            P("col"),
            P("row", "col"),
            P("col"),
            P("col", "row"),
            P("col"),
            P("col"),
            P("col"),
        ),
        check_vma=False,
    )
```

profile of v0, /device:TPU:0, one launch (start us, length us, event | category | flops | bytes accessed | tf_op | source)
XLA Modules:
  0.0 611.3 jit_solution(2286843427765584200)
XLA Ops:
  8.0 1.9 copy.31
  11.5 17.6 %all_gather.26 = bf16[256,1024]{1,0:T(8,128)(2,1)S(1)} all-gather(bf16[256,256]{1,0:T(8,128)(2,1)} %param.21), channel_id=1, replica_groups=mesh['dp'=2,'row'=4,'col'=4] {'row'}, dimensions={1}, use_global_device_ids=true | all-gather | bytes 655360 | tf_op jit(solution)/shard_map/all_gather | solution.py:108
  30.0 38.9 %all-gather.10.cloned.1.call-done = bf16[1024,3,256]{0,2,1:T(8,128)(2,1)} async-done(((bf16[256,3,256]{0,2,1:T(8,128)(2,1)}), bf16[1024,3,256]{0,2,1:T(8,128)(2,1)}) %all-gather.10.cloned.1.call-update) | async-done | bytes 1572880 | tf_op jit(solution)/shard_map/all_gather | solution.py:107
  69.0 2.7 fusion.26
  74.3 1.3 convolution_convert_fusion.5
  76.3 1.8 fusion.60
  78.8 28.9 %reduce-scatter.9.cloned.1.call-done = f32[512,256]{1,0:T(8,128)} async-done(((f32[512,1024]{1,0:T(8,128)}), f32[512,256]{1,0:T(8,128)}) %reduce-scatter.9.cloned.1.call-update) | async-done | bytes 524304 | tf_op jit(solution)/shard_map/reduce_scatter | solution.py:45
  108.9 5.8 psum.147
  114.9 5.7 psum.148
  122.1 32.7 %all-gather.14.cloned.1.call-done = bf16[1024,1024]{1,0:T(8,128)(2,1)} async-done(((bf16[256,1024]{1,0:T(8,128)(2,1)}), bf16[1024,1024]{1,0:T(8,128)(2,1)}) %all-gather.14.cloned.1.call-update) | async-done | bytes 2097168 | tf_op jit(solution)/shard_map/all_gather | solution.py:109
  154.8 17.6 %all-gather.12.cloned.1.call-done = bf16[512,1024]{1,0:T(8,128)(2,1)} async-done(((bf16[512,256]{1,0:T(8,128)(2,1)}), bf16[512,1024]{1,0:T(8,128)(2,1)}) %all-gather.12.cloned.1.call-update) | async-done | bytes 1048592 | tf_op jit(solution)/shard_map/all_gather | solution.py:37
  172.4 4.9 multiply_convert_fusion.1
  177.4 42.8 %all-gather.16.cloned.1.call-done = bf16[1024,1024]{1,0:T(8,128)(2,1)} async-done(((bf16[1024,256]{1,0:T(8,128)(2,1)}), bf16[1024,1024]{1,0:T(8,128)(2,1)}) %all-gather.16.cloned.1.call-update) | async-done | bytes 2097168 | tf_op jit(solution)/shard_map/all_gather | solution.py:110
  220.1 4.5 fusion.61
  224.7 29.4 %reduce-scatter.11.cloned.1.call-done = f32[512,256]{1,0:T(8,128)} async-done(((f32[512,1024]{1,0:T(8,128)}), f32[512,256]{1,0:T(8,128)}) %reduce-scatter.11.cloned.1.call-update) | async-done | bytes 524304 | tf_op jit(solution)/shard_map/reduce_scatter | solution.py:45
  254.2 1.3 fusion.52
  255.5 5.8 psum.149
  261.5 5.7 psum.150
  267.6 6.3 %all-reduce.2 = (f32[512]{0:T(512)S(1)}, f32[512]{0:T(512)S(1)}) all-reduce(f32[512]{0:T(512)S(1)} %get-tuple-element.84, f32[512]{0:T(512)S(1)} %get-tuple-element.87), channel_id=1, replica_groups=mesh['dp'=2,'row'=4,'col'=4] {'col'}, use_global_device_ids=true, to_apply=%region_15.16 | all-reduce | flops 1024 | bytes 8192 | tf_op jit(solution)/shard_map/psum | solution.py:32
  273.9 2.0 fusion.49
  276.9 17.4 %all-gather.18.cloned.1.call-done = bf16[512,1024]{1,0:T(8,128)(2,1)} async-done(((bf16[512,256]{1,0:T(8,128)(2,1)}), bf16[512,1024]{1,0:T(8,128)(2,1)}) %all-gather.18.cloned.1.call-update) | async-done | bytes 1048592 | tf_op jit(solution)/shard_map/all_gather | solution.py:41
  294.3 4.6 fusion.59
  299.9 2.6 fusion.38
  302.6 31.3 %reduce-scatter.13.cloned.1.call-done = f32[512,256]{1,0:T(8,128)} async-done(((f32[512,1024]{1,0:T(8,128)}), f32[512,256]{1,0:T(8,128)}) %reduce-scatter.13.cloned.1.call-update) | async-done | bytes 524304 | tf_op jit(solution)/shard_map/reduce_scatter | solution.py:49
  333.9 1.4 multiply_reduce_fusion.1
  335.3 5.8 all-reduce.1
  342.2 4.3 convolution_convert_fusion
  346.6 3.8 convolution_convert_fusion.1
  350.5 9.3 %all-gather.20.cloned.1.call-done = bf16[512,1024]{1,0:T(8,128)(2,1)} async-done(((bf16[512,256]{1,0:T(8,128)(2,1)}), bf16[512,1024]{1,0:T(8,128)(2,1)}) %all-gather.20.cloned.1.call-update) | async-done | bytes 1048592 | tf_op jit(solution)/shard_map/all_gather | solution.py:41
  359.8 1.8 convolution_convert_fusion.4
  362.3 4.1 fusion.55
  367.5 2.2 convolution_convert_fusion.3
  370.0 3.9 fusion.41
  373.9 8.8 %fusion.56 = (f32[4,64]{1,0:T(4,128)S(1)}, bf16[512,4,64]{0,2,1:T(8,128)(2,1)S(1)}) fusion(bf16[512,4,64]{0,2,1:T(8,128)(2,1)S(1)} %bitcast.55, f32[4,512,512]{1,2,0:T(8,128)} %fusion.41, f32[4,512]{1,0:T(4,128)S(1)} %log_add_fusion, f32[4,512,512]{1,2,0:T(8,128)} %copy-done, pred[512,512]{0,1:T(8,128)(4,1)S(1)} %broadcast_compare_fusion), kind=kOutput, calls=%fused_computation.90 | convolution fusion | flops 146016512 | bytes 9184256 | tf_op jit(solution)/shard_map/while/body/eval_jaxpr/hqk,khd->qhd/dot_general | solution.py:81
  382.9 7.5 %fusion.22 = bf16[4,64,512]{2,1,0:T(8,128)(2,1)S(1)} fusion(f32[4,512,512]{1,2,0:T(8,128)} %fusion.41, f32[512,4,64]{0,2,1:T(8,128)S(1)} %bitcast.51, f32[4,64]{1,0:T(4,128)S(1)} %add.163, f32[4,512,512]{1,2,0:T(8,128)} %copy-done, f32[4,512]{1,0:T(4,128)S(1)} %log_add_fusion, pred[512,512]{0,1:T(8,128)(4,1)S(1)} %broadcast_compare_fusion), kind=kOutput, calls=%fused_computation.28 | convolution fusion | flops 146147840 | bytes 9446400 | tf_op jit(solution)/shard_map/while/body/eval_jaxpr/hqk,qhd->khd/dot_general | solution.py:82
  390.6 2.2 fusion.18
  392.8 3.7 convolution_bitcast_fusion
  396.6 9.1 %reduce-scatter.23.cloned.1.call-done = bf16[1024,256]{1,0:T(8,128)(2,1)} async-done(((bf16[1024,1024]{1,0:T(8,128)(2,1)}), bf16[1024,256]{1,0:T(8,128)(2,1)}) %reduce-scatter.23.cloned.1.call-update) | async-done | bytes 524304 | tf_op jit(solution)/shard_map/reduce_scatter | solution.py:185
  405.7 45.0 %reduce-scatter.21.cloned.1.call-done = bf16[256,1024]{1,0:T(8,128)(2,1)} async-done(((bf16[1024,1024]{1,0:T(8,128)(2,1)}), bf16[256,1024]{1,0:T(8,128)(2,1)}) %reduce-scatter.21.cloned.1.call-update) | async-done | bytes 524304 | tf_op jit(solution)/shard_map/reduce_scatter | solution.py:182
  450.7 23.9 %reduce-scatter.19.cloned.1.call-done = bf16[256,256]{1,0:T(8,128)(2,1)} async-done(((bf16[256,1024]{1,0:T(8,128)(2,1)}), bf16[256,256]{1,0:T(8,128)(2,1)}) %reduce-scatter.19.cloned.1.call-update) | async-done | bytes 131088 | tf_op jit(solution)/shard_map/reduce_scatter | solution.py:179
  474.7 35.9 %reduce-scatter.17.cloned.1.call-done = bf16[256,3,256]{0,2,1:T(8,128)(2,1)} async-done(((bf16[1024,3,256]{0,2,1:T(8,128)(2,1)}), bf16[256,3,256]{0,2,1:T(8,128)(2,1)}) %reduce-scatter.17.cloned.1.call-update) | async-done | bytes 393232 | tf_op jit(solution)/shard_map/reduce_scatter | solution.py:176
  510.7 35.2 %all-reduce = (f32[256]{0:T(256)}, f32[256]{0:T(256)}, f32[256]{0:T(256)}, f32[256]{0:T(256)}, f32[256]{0:T(256)}, /*index=5*/f32[1024]{0:T(1024)}, f32[256]{0:T(256)}, f32[256]{0:T(256)}, f32[256]{0:T(256)}) all-reduce(f32[256]{0:T(256)S(1)} %reduce_sum.188, ...), channel_id=1, replica_groups=mesh['dp'=2,'row'=4,'col'=4] {'dp','row'}, use_global_device_ids=true, to_apply=%region_26.27 | all-reduce | flops 3072 | bytes 24576 | tf_op jit(solution)/shard_map/psum | solution.py:195
  546.0 1.9 add.185
  547.9 49.0 %all-reduce.6.cloned.1.call-done = (bf16[256,3,256]{0,2,1:T(8,128)(2,1)}, bf16[256,256]{1,0:T(8,128)(2,1)}, bf16[256,1024]{1,0:T(8,128)(2,1)}, bf16[1024,256]{1,0:T(8,128)(2,1)}) async-done(((bf16[256,3,256]{0,2,1:T(8,128)(2,1)}, bf16[256,256]{1,0:T(8,128)(2,1)}, bf16[256,1024]{1,0:T(8,128)(2,1)}, bf16[1024,256]{1,0:T(8,128)(2,1)}), (bf16[256,3,256]{0,2,1:T(8,128)(2,1)}, bf16[256,256]{1,0:T(8,128)(2,1)}, ...) | async-done | bytes 1572880 | tf_op jit(solution)/shard_map/psum | solution.py:190
  596.9 1.6 convert_element_type.113
  598.5 2.0 copy.41
  600.6 2.1 convert_element_type.115
  602.7 2.1 convert_element_type.117
  (100 shorter events, 16.8 us)
Async XLA Ops:
  7.2 22.9 %all-gather.8.cloned.1.call-start = ((), (), s32[]{:S(2)}) async-start(), calls=%async_computation.8 | async-start | bytes 1310720 | tf_op jit(solution)/shard_map/all_gather | solution.py:37
  7.9 61.1 %all-gather.10.cloned.1.call-start = ((), (), s32[]{:S(2)}) async-start(), calls=%async_computation.9 | async-start | bytes 1966080 | tf_op jit(solution)/shard_map/all_gather | solution.py:107
  9.9 97.8 %reduce-scatter.9.cloned.1.call-start = ((), (), s32[]{:S(2)}) async-start(), calls=%async_computation.10 | async-start | bytes 2621440 | tf_op jit(solution)/shard_map/reduce_scatter | solution.py:45
  71.8 0.7 copy-start.2
  73.4 2.2 copy-start
  75.6 0.7 copy-start.6
  75.6 32.1 %copy-start.4 = (bf16[512,256]{1,0:T(8,128)(2,1)S(1)}, bf16[512,256]{1,0:T(8,128)(2,1)}, u32[]{:S(2)}) copy-start(bf16[512,256]{1,0:T(8,128)(2,1)} %param.16) | copy-start | bytes 786436
  75.6 32.1 %copy-start.11 = (f32[256]{0:T(256)S(1)}, f32[256]{0:T(256)}, u32[]{:S(2)}) copy-start(f32[256]{0:T(256)} %param.22) | copy-start | bytes 3076
  75.6 44.9 %copy-start.8 = (f32[256]{0:T(256)S(1)}, f32[256]{0:T(256)}, u32[]{:S(2)}) copy-start(f32[256]{0:T(256)} %param.23) | copy-start | bytes 3076
  75.7 44.9 %copy-start.9 = (f32[256]{0:T(256)S(1)}, f32[256]{0:T(256)}, u32[]{:S(2)}) copy-start(f32[256]{0:T(256)} %param.24) | copy-start | bytes 3076
  76.3 96.1 %copy-start.17 = (f32[1024]{0:T(1024)S(1)}, f32[1024]{0:T(1024)}, u32[]{:S(2)}) copy-start(f32[1024]{0:T(1024)} %param.26) | copy-start | bytes 12292
  78.1 76.7 %all-gather.14.cloned.1.call-start = ((), (), s32[]{:S(2)}) async-start(), calls=%async_computation.12 | async-start | bytes 2621440 | tf_op jit(solution)/shard_map/all_gather | solution.py:109
  78.7 93.7 %all-gather.12.cloned.1.call-start = ((), (), s32[]{:S(2)}) async-start(), calls=%async_computation.11 | async-start | bytes 1310720 | tf_op jit(solution)/shard_map/all_gather | solution.py:37
  121.5 98.6 %all-gather.16.cloned.1.call-start = ((), (), s32[]{:S(2)}) async-start(), calls=%async_computation.13 | async-start | bytes 2621440 | tf_op jit(solution)/shard_map/all_gather | solution.py:110
  122.1 132.1 %reduce-scatter.11.cloned.1.call-start = ((), (), s32[]{:S(2)}) async-start(), calls=%async_computation.14 | async-start | bytes 2621440 | tf_op jit(solution)/shard_map/reduce_scatter | solution.py:45
  220.1 34.0 %copy-start.12 = (f32[256]{0:T(256)S(1)}, f32[256]{0:T(256)}, u32[]{:S(2)}) copy-start(f32[256]{0:T(256)} %param.28) | copy-start | bytes 3076
  220.1 47.0 %copy-start.5 = (bf16[512,256]{1,0:T(8,128)(2,1)S(1)}, bf16[512,256]{1,0:T(8,128)(2,1)}, u32[]{:S(2)}) copy-start(bf16[512,256]{1,0:T(8,128)(2,1)} %param.31) | copy-start | bytes 786436
  220.1 47.0 %copy-start.10 = (f32[256]{0:T(256)S(1)}, f32[256]{0:T(256)}, u32[]{:S(2)}) copy-start(f32[256]{0:T(256)} %param.29) | copy-start | bytes 3076
  224.6 49.3 %copy-start.13 = (f32[256]{0:T(256)S(1)}, f32[256]{0:T(256)}, u32[]{:S(2)}) copy-start(f32[256]{0:T(256)} %param.30) | copy-start | bytes 3076
  224.7 69.7 %all-gather.18.cloned.1.call-start = ((), (), s32[]{:S(2)}) async-start(), calls=%async_computation.15 | async-start | bytes 1310720 | tf_op jit(solution)/shard_map/all_gather | solution.py:41
  276.6 57.2 %reduce-scatter.13.cloned.1.call-start = ((), (), s32[]{:S(2)}) async-start(), calls=%async_computation.16 | async-start | bytes 2621440 | tf_op jit(solution)/shard_map/reduce_scatter | solution.py:49
  294.3 5.6 copy-start.14
  298.9 1.0 copy-start.18
  302.5 57.2 %all-gather.20.cloned.1.call-start = ((), (), s32[]{:S(2)}) async-start(), calls=%async_computation.17 | async-start | bytes 1310720 | tf_op jit(solution)/shard_map/all_gather | solution.py:41
  342.2 4.4 copy-start.16
  342.2 63.6 %reduce-scatter.23.cloned.1.call-start = ((), (), s32[]{:S(2)}) async-start(), calls=%async_computation.22 | async-start | bytes 2621440 | tf_op jit(solution)/shard_map/reduce_scatter | solution.py:185
  346.5 104.2 %reduce-scatter.21.cloned.1.call-start = ((), (), s32[]{:S(2)}) async-start(), calls=%async_computation.21 | async-start | bytes 2621440 | tf_op jit(solution)/shard_map/reduce_scatter | solution.py:182
  350.4 124.2 %reduce-scatter.19.cloned.1.call-start = ((), (), s32[]{:S(2)}) async-start(), calls=%async_computation.20 | async-start | bytes 655360 | tf_op jit(solution)/shard_map/reduce_scatter | solution.py:179
  359.8 7.7 %copy-start.1 = (bf16[512,1024]{1,0:T(8,128)(2,1)S(1)}, bf16[512,1024]{1,0:T(8,128)(2,1)}, u32[]{:S(2)}) copy-start(bf16[512,1024]{1,0:T(8,128)(2,1)} %all-gather.20.cloned.1.call-done) | copy-start | bytes 3145732
  361.6 0.7 copy-start.7
  366.4 7.5 %copy-start.3 = (bf16[512,1,256]{0,2,1:T(8,128)(2,1)S(1)}, bf16[512,1,256]{0,2,1:T(8,128)(2,1)}, u32[]{:S(2)}) copy-start(bf16[512,1,256]{0,2,1:T(8,128)(2,1)} %copy-done.2) | copy-start | bytes 786436
  369.8 140.8 %reduce-scatter.17.cloned.1.call-start = ((), (), s32[]{:S(2)}) async-start(), calls=%async_computation.19 | async-start | bytes 1966080 | tf_op jit(solution)/shard_map/reduce_scatter | solution.py:176
  382.9 7.7 %copy-start.15 = (bf16[512,1024]{1,0:T(8,128)(2,1)S(1)}, bf16[512,1024]{1,0:T(8,128)(2,1)}, u32[]{:S(2)}) copy-start(bf16[512,1024]{1,0:T(8,128)(2,1)} %all-gather.8.cloned.1.call-done) | copy-start | bytes 3145732
  392.8 153.2 %reduce-scatter.15.cloned.1.call-start = ((), (), s32[]{:S(2)}) async-start(), calls=%async_computation.18 | async-start | bytes 2621440 | tf_op jit(solution)/shard_map/reduce_scatter | solution.py:49
  396.6 200.3 %all-reduce.6.cloned.1.call-start = ((), (), s32[]{:S(2)}) async-start(), calls=%async_computation.23 | async-start | bytes 3145728 | tf_op jit(solution)/shard_map/psum | solution.py:190
Sparse Core Ops, SparseCore 0:
  9.5 19.5 all-gather.7
  31.2 37.6 all-gather.9
  78.3 29.3 reduce-scatter.8
  109.1 45.6 all-gather.13
  156.8 15.6 all-gather.11
  173.8 46.2 all-gather.15
  224.8 29.3 reduce-scatter.10
  276.8 17.5 all-gather.17
  302.6 31.1 reduce-scatter.12
  342.3 17.4 all-gather.19
  362.1 43.6 reduce-scatter.22
  407.9 42.8 reduce-scatter.20
  453.6 21.0 reduce-scatter.18
  476.8 33.6 reduce-scatter.16
  512.9 29.9 reduce-scatter.14
  545.3 51.5 all-reduce.5
where the time goes:
time: 612 us; the launch traced here: 611 us
  waiting for transfers between devices  413 us (67%)
  blocking collectives  87.8 us (14%)
  matrix products  65.8 us (11%)
  other arithmetic  19.2 us (3%)
  between operations  14.2 us (2%)
  local copies, waits for them, and re-layouts  10.1 us (2%)
    reduce_scatter x2, waiting for transfers between devices, collect(): return lax.psum_scatter(partial_sum, 'col', scatter_dimension=1, tiled=True)  58.4 us
    psum x1, waiting for transfers between devices, per_device(): lax.psum(pieces[0].astype(jnp.bfloat16), 'dp').astype(jnp.float32)  49 us
    reduce_scatter x1, waiting for transfers between devices, per_device(): lax.psum_scatter(wup_part.astype(jnp.bfloat16), 'row', scatter_dimension=...  45 us
    all_gather x1, waiting for transfers between devices, per_device(): lax.all_gather(w_down, 'row', axis=1, tiled=True)  42.8 us
    all_gather x1, waiting for transfers between devices, per_device(): lax.all_gather(w_qkv, 'row', axis=0, tiled=True)  38.9 us
    reduce_scatter x1, waiting for transfers between devices, per_device(): lax.psum_scatter(wqkv_part.astype(jnp.bfloat16), 'row', scatter_dimension...  35.9 us
    psum x1, blocking collectives, per_device(): lax.psum((qbias_part, vbias_part, obias_part, ngain_part, nshift_part, ub...  35.2 us
    all_gather x1, waiting for transfers between devices, per_device(): lax.all_gather(w_up, 'row', axis=0, tiled=True)  32.7 us
  transfers between devices with their start and end apart: 16, of which 14 were waited for; matrix products, arithmetic and copies ran while one was open for 9% of the time, Pallas kernels for 0%

commit v1 on v0

v1 whole, which is shorter than its diff:
```python
import functools

import jax
import jax.numpy as jnp
from jax import lax
from jax.experimental import pallas as pl
from jax.experimental.pallas import tpu as pltpu
from jax.sharding import PartitionSpec as P

HD = 64


EPS = 1e-12
INV_ROOT_TWO = 0.7071067811865476
INV_ROOT_PI = 0.3989422804014327


def gelu_parts(pre_act):
    cdf_val = 0.5 * (1.0 + lax.erf(pre_act * INV_ROOT_TWO))
    density = jnp.exp(-0.5 * pre_act * pre_act) * INV_ROOT_PI
    return (pre_act * cdf_val, cdf_val + pre_act * density)


def seq_scores(query, keys, doc_row):
    same_doc = doc_row[:, None] == doc_row[None, :]
    scores = jnp.einsum("qhd,khd->hqk", query, keys, preferred_element_type=jnp.float32) * HD ** (
        -0.5
    )
    return jnp.where(same_doc[None], scores, -jnp.inf)


def attend_seq(inputs_seq):
    query, keys, values, doc_row = inputs_seq
    scores = seq_scores(query, keys, doc_row)
    top_score = jnp.max(scores, axis=-1, keepdims=True)
    log_total = top_score + jnp.log(jnp.sum(jnp.exp(scores - top_score), axis=-1, keepdims=True))
    prob_bf = jnp.exp(scores - log_total).astype(jnp.bfloat16)
    context = jnp.einsum(
        "hqk,khd->qhd", prob_bf, values, preferred_element_type=jnp.float32
    ).astype(jnp.bfloat16)
    return (context, log_total)


def attend_back(inputs_seq):
    query, keys, values, doc_row, ctx_back, log_total = inputs_seq
    prob_f = jnp.exp(seq_scores(query, keys, doc_row) - log_total)
    v_back = jnp.einsum(
        "hqk,qhd->khd", prob_f.astype(jnp.bfloat16), ctx_back, preferred_element_type=jnp.float32
    )
    d_prob = jnp.einsum("qhd,khd->hqk", ctx_back, values, preferred_element_type=jnp.float32)
    row_delta = jnp.sum(prob_f * d_prob, axis=-1, keepdims=True)
    score_back = (prob_f * (d_prob - row_delta) * HD ** (-0.5)).astype(jnp.bfloat16)
    q_back = jnp.einsum("hqk,khd->qhd", score_back, keys, preferred_element_type=jnp.float32)
    k_back = jnp.einsum("hqk,qhd->khd", score_back, query, preferred_element_type=jnp.float32)
    return (q_back, k_back, v_back)


MESH = pl.DeviceIdType.MESH
VMEM = pl.BlockSpec(memory_space=pltpu.VMEM)
COST = pl.CostEstimate(flops=0, bytes_accessed=30_000_000, transcendentals=0)


def remote(src, dst, send_sem, recv_sem, target):
    return pltpu.make_async_remote_copy(
        src_ref=src,
        dst_ref=dst,
        send_sem=send_sem,
        recv_sem=recv_sem,
        device_id={"col": target},
        device_id_type=MESH,
    )


def place(count):
    me = lax.axis_index("col")
    chip, core = lax.div(me, 2), lax.rem(me, 2)
    return me, chip, core, chip * 2 + 1 - core


def greet(count, me):
    barrier = pltpu.get_barrier_semaphore()
    for step in range(1, count):
        pl.semaphore_signal(
            barrier,
            inc=1,
            device_id={"col": lax.rem(me + step, count)},
            device_id_type=MESH,
        )
    pl.semaphore_wait(barrier, count - 1)


def rows_of(index, size):
    return pl.ds(pl.multiple_of(index * size, size), size)


def start_reduce(count, view, slots, sums, s1, r1, s2, r2):
    me, chip, core, partner = place(count)
    chips = count // 2
    far = lambda step: lax.rem(chip + step, chips)
    order = list(range(1, chips)) + [0]
    first = {}
    for step in order:
        first[step] = remote(
            view(far(step) * 2 + 1 - core), slots.at[step], s1.at[step], r1.at[step], partner
        )
        first[step].start()
    second = {}
    for step in range(1, chips):
        first[step].wait_recv()
        owner = far(step) * 2 + core
        sums[step] = (
            view(owner)[...].astype(jnp.float32) + slots[step].astype(jnp.float32)
        ).astype(jnp.bfloat16)
        second[step] = remote(
            sums.at[step], sums.at[chips + step], s2.at[step], r2.at[step], owner
        )
        second[step].start()
    first[0].wait_recv()
    return first, second


def finish_reduce(count, view, slots, sums, pending):
    first, second = pending
    me = lax.axis_index("col")
    chips = count // 2
    total = view(me)[...].astype(jnp.float32) + slots[0].astype(jnp.float32)
    for step in range(1, chips):
        second[step].wait_recv()
        total = total + sums[chips + step].astype(jnp.float32)
    for copy in list(first.values()) + list(second.values()):
        copy.wait_send()
    return total


def gather_blocks(count, source, view, s3, r3, s4, r4):
    me, chip, core, partner = place(count)
    chips = count // 2
    sent = []
    for step in range(1, chips):
        peer = lax.rem(chip + step, chips) * 2 + core
        sent.append(remote(source, view(me), s3.at[step], r3.at[step], peer))
        sent[-1].start()
    near = remote(source, view(me), s3.at[0], r3.at[0], partner)
    near.start()
    return sent, near


def gather_rest(count, view, pending, s4, r4):
    me, chip, core, partner = place(count)
    chips = count // 2
    sent, near = pending
    passed = []
    for step in range(1, chips):
        origin = lax.rem(chip + chips - step, chips) * 2 + core
        sent[step - 1].wait_recv()
        passed.append(remote(view(origin), view(origin), s4.at[step], r4.at[step], partner))
        passed[-1].start()
    near.wait_recv()
    for copy in passed:
        copy.wait_recv()
    for copy in sent + [near] + passed:
        copy.wait_send()


def spread_kernel(count, x_ref, og_ref, par_ref, full_ref, og_out, par_out, *sems):
    s3, r3, s4, r4, sa, ra, sb, rb = sems
    me = lax.axis_index("col")
    width = x_ref.shape[1]
    rows = og_ref.shape[0] // count
    greet(count, me)
    view = lambda index: full_ref.at[:, rows_of(index, width)]
    pending = gather_blocks(count, x_ref, view, s3, r3, s4, r4)
    mine = rows_of(me, width)
    others = []
    for step in range(1, count):
        target = lax.rem(me + step, count)
        others.append(
            remote(og_ref.at[rows_of(target, rows), :], og_out.at[:, mine], sa.at[step], ra.at[step], target)
        )
        others.append(remote(par_ref, par_out.at[:, mine], sb.at[step], rb.at[step], target))
    for copy in others:
        copy.start()
    full_ref[:, mine] = x_ref[...]
    og_out[:, mine] = og_ref[rows_of(me, rows), :]
    par_out[:, mine] = par_ref[...]
    gather_rest(count, view, pending, s4, r4)
    for copy in others:
        copy.wait()


def spread_all(count, x, og, par):
    tokens, width = x.shape
    dma = pltpu.SemaphoreType.DMA
    return pl.pallas_call(
        functools.partial(spread_kernel, count),
        out_shape=(
            jax.ShapeDtypeStruct((tokens, width * count), x.dtype),
            jax.ShapeDtypeStruct((tokens // count, width * count), og.dtype),
            jax.ShapeDtypeStruct((par.shape[0], width * count), par.dtype),
        ),
        in_specs=[VMEM] * 3,
        out_specs=(VMEM,) * 3,
        scratch_shapes=[dma((count,))] * 8,
        compiler_params=pltpu.CompilerParams(collective_id=0, has_side_effects=True),
        cost_estimate=COST,
    )(x, og, par)


def middle_kernel(count, mid, n_aux, n_out, exchange, *refs):
    part = refs[0]
    aux = refs[1 : 1 + n_aux]
    full = refs[1 + n_aux]
    outs = refs[2 + n_aux : 2 + n_aux + n_out]
    slots, sums, swap, s1, r1, s2, r2, s3, r3, s4, r4, sa, ra = refs[2 + n_aux + n_out :]
    me = lax.axis_index("col")
    rows = part.shape[0] // count
    greet(count, me)
    view = lambda index: part.at[rows_of(index, rows), :]
    pending = start_reduce(count, view, slots, sums, s1, r1, s2, r2)
    total = finish_reduce(count, view, slots, sums, pending)
    mid(total, me, aux, outs, full.at[rows_of(me, rows), :], swap)
    out_view = lambda index: full.at[rows_of(index, rows), :]
    pending = gather_blocks(count, out_view(me), out_view, s3, r3, s4, r4)
    others = []
    if exchange:
        laid = outs[0]
        width = laid.shape[1]
        for step in range(1, count):
            target = lax.rem(me + step, count)
            others.append(
                remote(
                    swap.at[:, rows_of(target, width)],
                    laid.at[rows_of(me, rows), :],
                    sa.at[step],
                    ra.at[step],
                    target,
                )
            )
            others[-1].start()
        laid[rows_of(me, rows), :] = swap[:, rows_of(me, width)]
    gather_rest(count, out_view, pending, s4, r4)
    for copy in others:
        copy.wait()


def middle(count, part, aux, mid, outs, exchange, cid):
    tokens, width = part.shape
    rows = tokens // count
    dma = pltpu.SemaphoreType.DMA
    return pl.pallas_call(
        functools.partial(middle_kernel, count, mid, len(aux), len(outs), exchange),
        out_shape=(jax.ShapeDtypeStruct((tokens, width), jnp.bfloat16),) + tuple(outs),
        in_specs=[VMEM] * (1 + len(aux)),
        out_specs=(VMEM,) * (1 + len(outs)),
        scratch_shapes=[
            pltpu.VMEM((count // 2, rows, width), jnp.bfloat16),
            pltpu.VMEM((count, rows, width), jnp.bfloat16),
            pltpu.VMEM((rows, width), jnp.bfloat16),
        ]
        + [dma((count,))] * 10,
        compiler_params=pltpu.CompilerParams(collective_id=cid, has_side_effects=True),
        cost_estimate=COST,
    )(part, *aux)


def last_kernel(count, part, back_full, out, slots, sums, s1, r1, s2, r2):
    me = lax.axis_index("col")
    width = part.shape[1] // count
    greet(count, me)
    view = lambda index: part.at[:, rows_of(index, width)]
    pending = start_reduce(count, view, slots, sums, s1, r1, s2, r2)
    total = finish_reduce(count, view, slots, sums, pending)
    out[...] = total + back_full[:, rows_of(me, width)].astype(jnp.float32)


def last(count, part, back_full):
    tokens, width = part.shape
    cols = width // count
    dma = pltpu.SemaphoreType.DMA
    return pl.pallas_call(
        functools.partial(last_kernel, count),
        out_shape=jax.ShapeDtypeStruct((tokens, cols), jnp.float32),
        in_specs=[VMEM] * 2,
        out_specs=VMEM,
        scratch_shapes=[
            pltpu.VMEM((count // 2, tokens, cols), jnp.bfloat16),
            pltpu.VMEM((count, tokens, cols), jnp.bfloat16),
        ]
        + [dma((count,))] * 4,
        compiler_params=pltpu.CompilerParams(collective_id=4, has_side_effects=True),
        cost_estimate=COST,
    )(part, back_full)


def norm_parts(total):
    mean_val = jnp.mean(total, axis=1, keepdims=True)
    centered = total - mean_val
    inverse = lax.rsqrt(jnp.mean(centered * centered, axis=1, keepdims=True) + EPS)
    return centered * inverse, inverse


def norm_back(upstream, normed, inverse, gain):
    scaled = upstream * gain
    first = jnp.mean(scaled, axis=1, keepdims=True)
    second = jnp.mean(scaled * normed, axis=1, keepdims=True)
    return inverse * (scaled - first - normed * second)


def column_sum(values):
    return jnp.sum(values, axis=0, keepdims=True)


def mid_one(total, me, aux, outs, block, swap):
    x_full, par = aux
    act_out, normed_out, inverse_out = outs
    rows = total.shape[0]
    total = x_full[rows_of(me, rows), :].astype(jnp.float32) + (total + par[0:1, :])
    normed, inverse = norm_parts(total)
    act = normed * par[1:2, :] + par[2:3, :]
    act_out[...] = act
    normed_out[...] = normed
    inverse_out[...] = jnp.broadcast_to(inverse, inverse_out.shape)
    block[...] = act.astype(jnp.bfloat16)


def mid_two(total, me, aux, outs, block, swap):
    act, grad, par = aux
    laid, back_out, sum_out = outs
    total = act[...] + (total + par[3:4, :])
    normed, inverse = norm_parts(total)
    gain = par[4:5, :]
    swap[...] = (normed * gain + par[5:6, :]).astype(jnp.bfloat16)
    top = grad[...].astype(jnp.float32)
    back = norm_back(top, normed, inverse, gain)
    back_out[...] = back
    sum_out[0:1, :] = column_sum(top * normed)
    sum_out[1:2, :] = column_sum(top)
    sum_out[2:3, :] = column_sum(back)
    block[...] = back.astype(jnp.bfloat16)


def mid_three(total, me, aux, outs, block, swap):
    back_two, normed_ref, inverse, par = aux
    (sum_out,) = outs
    upstream = back_two[...] + total
    normed = normed_ref[...]
    back = norm_back(upstream, normed, inverse[:, 0:1], par[1:2, :])
    sum_out[0:1, :] = column_sum(upstream * normed)
    sum_out[1:2, :] = column_sum(upstream)
    sum_out[2:3, :] = column_sum(back)
    block[...] = back.astype(jnp.bfloat16)


def ring_gather(block, axis, count):
    me = lax.axis_index("row")
    ring = [(i, (i + 1) % count) for i in range(count)]
    size = block.shape[axis]
    shape = list(block.shape)
    shape[axis] = size * count
    whole = jnp.zeros(shape, block.dtype)
    for step in range(count):
        whole = lax.dynamic_update_slice_in_dim(
            whole, block, lax.rem(me - step + count, count) * size, axis
        )
        if step < count - 1:
            block = lax.ppermute(block, "row", ring)
    return whole


def ring_scatter(part, axis, count):
    me = lax.axis_index("row")
    ring = [(i, (i + 1) % count) for i in range(count)]
    size = part.shape[axis] // count

    def own(step):
        owner = lax.rem(me - 1 - step + 2 * count, count)
        return lax.dynamic_slice_in_dim(part, owner * size, size, axis)

    total = own(0).astype(jnp.bfloat16)
    for step in range(1, count):
        moved = lax.ppermute(total, "row", ring)
        total = (moved.astype(jnp.float32) + own(step).astype(jnp.float32)).astype(jnp.bfloat16)
    return total


def pair_sum(total, count):
    result = total.astype(jnp.float32)
    moved = total
    ring = [(i, (i + 1) % count) for i in range(count)]
    if count == 2:
        return result + lax.ppermute(moved, "dp", ring).astype(jnp.float32)
    return lax.psum(total, "dp").astype(jnp.float32)


def per_device(
    rows_n,
    cols_n,
    dp_n,
    hidden_in,
    doc_ids,
    w_qkv,
    query_bias,
    value_bias,
    w_out,
    out_bias,
    norm_gain,
    norm_shift,
    w_up,
    up_bias,
    w_down,
    down_bias,
    final_gain,
    final_shift,
    out_grad,
):
    f32 = jnp.float32
    bf16 = jnp.bfloat16
    tokens_dev = hidden_in.shape[0]
    col_width = hidden_in.shape[1]
    head_count = col_width // HD
    seq_count = doc_ids.shape[0]
    seq_len = doc_ids.shape[1]
    head_shape = (seq_count, seq_len, head_count, HD)
    width = col_width * cols_n
    part_rows = tokens_dev // cols_n
    qkv_full = ring_gather(w_qkv.reshape(w_qkv.shape[0], -1), 0, rows_n)
    out_full = ring_gather(w_out, 1, rows_n)
    up_full = ring_gather(w_up, 0, rows_n)
    down_full = ring_gather(w_down, 1, rows_n)
    blank = jnp.zeros_like(out_bias)
    par = jnp.stack(
        [out_bias, norm_gain, norm_shift, down_bias, final_gain, final_shift, blank, blank]
    )
    x_full, top_rows, par_full = spread_all(cols_n, hidden_in, out_grad, par)
    projected = jnp.dot(x_full, qkv_full, preferred_element_type=f32)
    query = (projected[:, :col_width] + query_bias).astype(bf16).reshape(head_shape)
    keys = projected[:, col_width : 2 * col_width].astype(bf16).reshape(head_shape)
    values = (projected[:, 2 * col_width :] + value_bias).astype(bf16).reshape(head_shape)
    context, log_total = lax.map(attend_seq, (query, keys, values, doc_ids))
    ctx_rows = context.reshape(tokens_dev, col_width)
    block_f32 = jax.ShapeDtypeStruct((part_rows, width), f32)
    sums_f32 = jax.ShapeDtypeStruct((8, width), f32)
    attn_full, attn_act, normed_one, inverse_one = middle(
        cols_n,
        jnp.dot(ctx_rows, out_full, preferred_element_type=f32).astype(bf16),
        (x_full, par_full),
        mid_one,
        (block_f32, block_f32, jax.ShapeDtypeStruct((part_rows, 128), f32)),
        False,
        1,
    )
    up_pre = jnp.dot(attn_full, up_full, preferred_element_type=f32) + up_bias
    act_f, slope = gelu_parts(up_pre)
    act = act_f.astype(bf16)
    back_two_full, layer_out, back_two, sums_two = middle(
        cols_n,
        jnp.dot(act, down_full, preferred_element_type=f32).astype(bf16),
        (attn_act, top_rows, par_full),
        mid_two,
        (jax.ShapeDtypeStruct((tokens_dev, col_width), bf16), block_f32, sums_f32),
        True,
        2,
    )
    up_back = jnp.dot(back_two_full, down_full.T, preferred_element_type=f32) * slope
    up_back_bf = up_back.astype(bf16)
    back_one_full, sums_one = middle(
        cols_n,
        jnp.dot(up_back_bf, up_full.T, preferred_element_type=f32).astype(bf16),
        (back_two, normed_one, inverse_one, par_full),
        mid_three,
        (sums_f32,),
        False,
        3,
    )
    wdown_part = jnp.dot(act.T, back_two_full, preferred_element_type=f32).astype(bf16)
    wdown_grad = pair_sum(ring_scatter(wdown_part, 1, rows_n), dp_n)
    wup_part = jnp.dot(attn_full.T, up_back_bf, preferred_element_type=f32).astype(bf16)
    wup_grad = pair_sum(ring_scatter(wup_part, 0, rows_n), dp_n)
    ubias_part = jnp.sum(up_back, axis=0)
    wout_part = jnp.dot(ctx_rows.T, back_one_full, preferred_element_type=f32).astype(bf16)
    wout_grad = pair_sum(ring_scatter(wout_part, 1, rows_n), dp_n)
    ctx_back = (
        jnp.dot(back_one_full, out_full.T, preferred_element_type=f32)
        .astype(bf16)
        .reshape(head_shape)
    )
    q_back, k_back, v_back = lax.map(
        attend_back, (query, keys, values, doc_ids, ctx_back, log_total)
    )
    q_back = q_back.reshape(tokens_dev, col_width)
    k_back = k_back.reshape(tokens_dev, col_width)
    v_back = v_back.reshape(tokens_dev, col_width)
    qbias_part = jnp.sum(q_back, axis=0)
    vbias_part = jnp.sum(v_back, axis=0)
    qkv_back = jnp.concatenate([q_back.astype(bf16), k_back.astype(bf16), v_back.astype(bf16)], axis=1)
    wqkv_part = jnp.dot(x_full.T, qkv_back, preferred_element_type=f32).astype(bf16)
    wqkv_grad = pair_sum(ring_scatter(wqkv_part, 0, rows_n), dp_n).reshape(w_qkv.shape)
    hidden_grad = last(
        cols_n,
        jnp.dot(qkv_back, qkv_full.T, preferred_element_type=f32).astype(bf16),
        back_one_full,
    )
    six = lax.psum(jnp.concatenate([sums_two[:3], sums_one[:3]], axis=0), ("dp", "row", "col"))
    six = lax.dynamic_slice_in_dim(six, lax.axis_index("col") * col_width, col_width, 1)
    local = lax.psum(jnp.concatenate([ubias_part, qbias_part, vbias_part]), ("dp", "row"))
    hidden_w = ubias_part.shape[0]
    return (
        layer_out,
        hidden_grad,
        wqkv_grad,
        local[hidden_w : hidden_w + col_width],
        local[hidden_w + col_width :],
        wout_grad,
        six[5],
        six[3],
        six[4],
        wup_grad,
        local[:hidden_w],
        wdown_grad,
        six[2],
        six[0],
        six[1],
    )


def solution(mesh):
    placed = (
        P(("dp", "row"), "col"),
        P(("dp", "row"), None),
        P("row", None, "col"),
        P("col"),
        P("col"),
        P("col", "row"),
        P("col"),
        P("col"),
        P("col"),
        P("row", "col"),
        P("col"),
        P("col", "row"),
        P("col"),
        P("col"),
        P("col"),
        P(("dp", "row"), "col"),
    )
    return jax.shard_map(
        functools.partial(per_device, mesh.shape["row"], mesh.shape["col"], mesh.shape["dp"]),
        mesh=mesh,
        in_specs=placed,
        out_specs=(
            P(("dp", "row"), "col"),
            P(("dp", "row"), "col"),
            P("row", None, "col"),
            P("col"),
            P("col"),
            P("col", "row"),
            P("col"),
            P("col"),
            P("col"),
            P("row", "col"),
            P("col"),
            P("col", "row"),
            P("col"),
            P("col"),
            P("col"),
        ),
        check_vma=False,
    )
```

time: 612 us -> 403 us (0.66)
  waiting for transfers between devices: 413 us -> 118 us
  Pallas kernels: 0 us -> 93.9 us
  starting transfers between devices: 1.05 us -> 28.9 us
  blocking collectives: 87.8 us -> 68.1 us
  local copies, waits for them, and re-layouts: 10.1 us -> 28.9 us
  between operations: 14.2 us -> 1.53 us
  matrix products: 65.8 us -> 54.2 us
  other arithmetic: 19.2 us -> 8.85 us
    reduce_scatter x8 -> x0, waiting for transfers between devices: 204 us -> none  [the longest x2 58.4 us: collect(): return lax.psum_scatter(partial_sum, 'col', scatter_dimension=1, tiled=True)]
    all_gather x7 -> x0, waiting for transfers between devices: 159 us -> none  [the longest x1 42.8 us: per_device(): lax.all_gather(w_down, 'row', axis=1, tiled=True)]
    ppermute x0 -> x28, waiting for transfers between devices: none -> 118 us  [the longest x12 56 us: ring_scatter(): moved = lax.ppermute(total, 'row', ring)]
    pallas_call x0 -> x5, Pallas kernels: none -> 93.9 us  [the longest x3 67.7 us: middle(): pl.pallas_call(functools.partial(middle_kernel, count, mid, len(aux), len...]
    psum x1 -> x0, waiting for transfers between devices: 49 us -> none  [per_device(): lax.psum(pieces[0].astype(jnp.bfloat16), 'dp').astype(jnp.float32)]
    ppermute x0 -> x28, starting transfers between devices: none -> 28.9 us  [the longest x12 11.4 us: ring_gather(): block = lax.ppermute(block, 'row', ring)]
    all_gather x1 -> x0, blocking collectives: 17.6 us -> none  [per_device(): lax.all_gather(w_out, 'row', axis=1, tiled=True)]
    dynamic_update_slice x0 -> x16, local copies, waits for them, and re-layouts: none -> 11.8 us  [ring_gather(): lax.dynamic_update_slice_in_dim(whole, block, lax.rem(me - step + count,...]
  transfers between devices with their start and end apart: 16 -> 28, of which waited for: 14 -> 16; matrix products, arithmetic and copies ran while one was open for 9% -> 9% of each run, Pallas kernels for 0% -> 9%
where the time goes in v1:
time: 403 us; the launch traced here: 402 us
  waiting for transfers between devices  118 us (29%)
  Pallas kernels  93.9 us (23%)
  blocking collectives  68.1 us (17%)
  matrix products  54.2 us (13%)
  local copies, waits for them, and re-layouts  28.9 us (7%)
  starting transfers between devices  28.9 us (7%)
  other arithmetic  8.85 us (2%)
    pallas_call x3, Pallas kernels, middle(): pl.pallas_call(functools.partial(middle_kernel, count, mid, len(aux), len...  67.7 us
    ppermute x12, waiting for transfers between devices, ring_scatter(): moved = lax.ppermute(total, 'row', ring)  56 us
    ppermute x12, waiting for transfers between devices, ring_gather(): block = lax.ppermute(block, 'row', ring)  53.8 us
    psum x1, blocking collectives, per_device(): lax.psum(jnp.concatenate([sums_two[:3], sums_one[:3]], axis=0), ('dp', 'r...  49.8 us
    psum x1, blocking collectives, per_device(): lax.psum(jnp.concatenate([ubias_part, qbias_part, vbias_part]), ('dp', 'r...  18.3 us
    pallas_call x1, Pallas kernels, spread_all(): pl.pallas_call(functools.partial(spread_kernel, count), out_shape=(jax.Sh...  13.4 us
    pallas_call x1, Pallas kernels, last(): pl.pallas_call(functools.partial(last_kernel, count), out_shape=jax.Shape...  12.7 us
    dynamic_update_slice x16, local copies, waits for them, and re-layouts, ring_gather(): lax.dynamic_update_slice_in_dim(whole, block, lax.rem(me - step + count,...  11.8 us
  transfers between devices with their start and end apart: 28, of which 16 were waited for; matrix products, arithmetic and copies ran while one was open for 9% of the time, Pallas kernels for 9%

profile of v1, /device:TPU:0, one launch (start us, length us, event | category | flops | bytes accessed | tf_op | source)
XLA Modules:
  0.0 402.5 jit_solution(3803621886409532266)
XLA Ops:
  1.9 3.1 collective-permute-start
  9.9 9.9 %collective-permute-done.3 = bf16[256,256]{1,0:T(8,128)(2,1)S(1)} collective-permute-done((bf16[256,256]{1,0:T(8,128)(2,1)}, bf16[256,256]{1,0:T(8,128)(2,1)S(1)}, u32[]{:S(2)}, u32[]{:S(2)}) %collective-permute-start.3) | collective-permute-done | bytes 131104 | tf_op jit(solution)/shard_map/ppermute | solution.py:366
  20.6 13.4 %shard_map.271 = (bf16[512,1024]{1,0:T(8,128)(2,1)}, bf16[128,1024]{1,0:T(8,128)(2,1)}, f32[8,1024]{1,0:T(8,128)}) custom-call(bf16[512,256]{1,0:T(8,128)(2,1)} %x_ref.1, bf16[512,256]{1,0:T(8,128)(2,1)} %og_ref.1, f32[8,256]{1,0:T(8,128)} %stack.31.par_ref), custom_call_target="tpu_custom_call" | custom-call | bytes 30000000 | tf_op jit(solution)/shard_map/pallas_call | solution.py:194
  35.6 8.6 %collective-permute-done.4 = bf16[256,256]{1,0:T(8,128)(2,1)S(1)} collective-permute-done((bf16[256,256]{1,0:T(8,128)(2,1)S(1)}, bf16[256,256]{1,0:T(8,128)(2,1)S(1)}, u32[]{:S(2)}, u32[]{:S(2)}) %collective-permute-start.4) | collective-permute-done | bytes 131104 | tf_op jit(solution)/shard_map/ppermute | solution.py:366
  45.6 1.6 collective-permute-start.7
  47.2 2.1 collective-permute-start.10
  49.3 3.1 collective-permute-done.5
  53.5 1.9 constant_dynamic-update-slice_fusion.6
  55.3 5.5 %collective-permute-done.1 = bf16[256,768]{0,1:T(8,128)(2,1)S(1)} collective-permute-done((bf16[256,768]{0,1:T(8,128)(2,1)}, bf16[256,768]{0,1:T(8,128)(2,1)S(1)}, u32[]{:S(2)}, u32[]{:S(2)}) %collective-permute-start.1) | collective-permute-done | bytes 393248 | tf_op jit(solution)/shard_map/ppermute | solution.py:366
  62.0 10.2 %collective-permute-done.7 = bf16[256,1024]{1,0:T(8,128)(2,1)} collective-permute-done((bf16[256,1024]{1,0:T(8,128)(2,1)}, bf16[256,1024]{1,0:T(8,128)(2,1)}, u32[]{:S(2)}, u32[]{:S(2)}) %collective-permute-start.7) | collective-permute-done | bytes 524320 | tf_op jit(solution)/shard_map/ppermute | solution.py:366
  72.2 11.2 %collective-permute-done.10 = bf16[1024,256]{1,0:T(8,128)(2,1)} collective-permute-done((bf16[1024,256]{1,0:T(8,128)(2,1)}, bf16[1024,256]{1,0:T(8,128)(2,1)}, u32[]{:S(2)}, u32[]{:S(2)}) %collective-permute-start.10) | collective-permute-done | bytes 524320 | tf_op jit(solution)/shard_map/ppermute | solution.py:366
  83.4 1.9 constant_dynamic-update-slice_fusion.5
  86.4 5.3 %collective-permute-done.2 = bf16[256,768]{0,1:T(8,128)(2,1)S(1)} collective-permute-done((bf16[256,768]{0,1:T(8,128)(2,1)S(1)}, bf16[256,768]{0,1:T(8,128)(2,1)S(1)}, u32[]{:S(2)}, u32[]{:S(2)}) %collective-permute-start.2) | collective-permute-done | bytes 393248 | tf_op jit(solution)/shard_map/ppermute | solution.py:366
  102.8 22.6 %shard_map.272 = (bf16[512,1024]{1,0:T(8,128)(2,1)}, f32[128,1024]{1,0:T(8,128)}, f32[128,1024]{1,0:T(8,128)}, f32[128,128]{1,0:T(8,128)}) custom-call(bf16[512,1024]{1,0:T(8,128)(2,1)} %convolution_convert_fusion.6.refs_0_, bf16[512,1024]{1,0:T(8,128)(2,1)} %get-tuple-element.79.refs_1_, f32[8,1024]{1,0:T(8,128)} %get-tuple-element.80.refs_2_.refs_3_.refs_4_), custom_call_target="tpu_custom_call" | custom-call | bytes 30000000 | tf_op jit(solution)/shard_map/pallas_call | solution.py:250
  125.4 1.9 constant_dynamic-update-slice_fusion.4
  127.3 4.6 %multiply_convert_fusion.1 = (bf16[512,1024]{1,0:T(8,128)(2,1)S(1)}, f32[512,1024]{1,0:T(8,128)}) fusion(f32[1024]{0:T(1024)S(1)} %copy-done.32, bf16[512,1024]{1,0:T(8,128)(2,1)} %get-tuple-element.81, bf16[1024,1024]{1,0:T(8,128)(2,1)} %constant_dynamic-update-slice_fusion.4), kind=kOutput, calls=%fused_computation.16 | convolution fusion | flops 1076887552 | bytes 6295552 | tf_op jit(solution)/shard_map/dot_general | solution.py:452
  133.4 2.2 convolution_convert_fusion.5.refs_0_
  135.6 22.7 %shard_map.273 = (bf16[512,1024]{1,0:T(8,128)(2,1)}, bf16[512,256]{1,0:T(8,128)(2,1)}, f32[128,1024]{1,0:T(8,128)}, f32[8,1024]{1,0:T(8,128)}) custom-call(bf16[512,1024]{1,0:T(8,128)(2,1)} %convolution_convert_fusion.5.refs_0_, f32[128,1024]{1,0:T(8,128)} %get-tuple-element.82.refs_1_, bf16[128,1024]{1,0:T(8,128)(2,1)} %get-tuple-element.83.refs_2_, ...), custom_call_target="tpu_custom_call" | custom-call | bytes 30000000 | tf_op jit(solution)/shard_map/pallas_call | solution.py:250
  158.3 4.0 fusion.42
  162.3 2.3 convolution_convert_fusion.4.refs_0_
  164.5 22.5 %shard_map.274 = (bf16[512,1024]{1,0:T(8,128)(2,1)}, f32[8,1024]{1,0:T(8,128)}) custom-call(bf16[512,1024]{1,0:T(8,128)(2,1)} %convolution_convert_fusion.4.refs_0_, f32[128,1024]{1,0:T(8,128)} %get-tuple-element.86.refs_1_, f32[128,1024]{1,0:T(8,128)} %get-tuple-element.87.refs_2_, f32[128,128]{1,0:T(8,128)} %get-tuple-element.88.refs_3_, ...), custom_call_target="tpu_custom_call" | custom-call | bytes 30000000 | tf_op jit(solution)/shard_map/pallas_call | solution.py:250
  187.0 1.7 convolution_convert_fusion.8
  188.7 3.5 fusion.37
  192.2 2.7 fusion.44
  194.9 8.1 %fusion.21 = bf16[4,64,512]{2,1,0:T(8,128)(2,1)} fusion(bf16[512,4,64]{0,2,1:T(8,128)(2,1)S(1)} %bitcast.71, f32[4,512,512]{1,2,0:T(8,128)} %fusion.44, f32[4,512,512]{1,2,0:T(8,128)} %copy-done, f32[4,512]{1,0:T(4,128)S(1)} %log_add_fusion, pred[512,512]{0,1:T(8,128)(4,1)S(1)} %broadcast_compare_fusion), kind=kOutput, calls=%fused_computation.30 | convolution fusion | flops 145885696 | bytes 9183232 | tf_op jit(solution)/shard_map/while/body/eval_jaxpr/hqk,qhd->khd/dot_general | solution.py:54
  203.0 9.4 %fusion.36 = (f32[4,64]{1,0:T(4,128)S(1)}, bf16[512,4,64]{0,2,1:T(8,128)(2,1)}) fusion(bf16[512,4,64]{0,2,1:T(8,128)(2,1)S(1)} %bitcast.67, f32[4,512,512]{1,2,0:T(8,128)} %fusion.44, f32[4,512]{1,0:T(4,128)S(1)} %log_add_fusion, f32[4,512,512]{1,2,0:T(8,128)} %copy-done, pred[512,512]{0,1:T(8,128)(4,1)S(1)} %broadcast_compare_fusion), kind=kOutput, calls=%fused_computation.90 | convolution fusion | flops 146016512 | bytes 9184256 | tf_op jit(solution)/shard_map/while/body/eval_jaxpr/hqk,khd->qhd/dot_general | solution.py:53
  212.4 3.1 convolution_convert_fusion.3.part
  215.6 2.1 convolution_convert_fusion.2
  219.7 18.3 %psum.14 = f32[1536]{0:T(1024)S(1)} all-reduce(f32[1536]{0:T(1024)S(1)} %pad_maximum_fusion.4), channel_id=1, replica_groups=mesh['dp'=2,'row'=4,'col'=4] {'dp','row'}, use_global_device_ids=true, to_apply=%region_6.7 | all-reduce | flops 1536 | bytes 12288 | tf_op jit(solution)/shard_map/psum | solution.py:505
  239.2 4.2 %convolution_convert_fusion = bf16[1024,1024]{1,0:T(8,128)(2,1)} fusion(bf16[512,1024]{1,0:T(8,128)(2,1)} %copy-done.35, bf16[512,1024]{1,0:T(8,128)(2,1)} %get-tuple-element.85), kind=kOutput, calls=%fused_computation.20 | convolution fusion | flops 1074790400 | bytes 4194304 | tf_op jit(solution)/shard_map/dot_general | solution.py:475
  243.3 12.7 %shard_map.275 = f32[512,256]{1,0:T(8,128)} custom-call(bf16[512,1024]{1,0:T(8,128)(2,1)} %convolution_convert_fusion.3.part, bf16[512,1024]{1,0:T(8,128)(2,1)} %get-tuple-element.89.back_full), custom_call_target="tpu_custom_call" | custom-call | bytes 30000000 | tf_op jit(solution)/shard_map/pallas_call | solution.py:280
  256.0 1.8 constant_dynamic-slice_fusion.4
  261.1 1.9 constant_dynamic-slice_fusion.1
  263.0 2.5 collective-permute-start.24
  265.6 49.8 %psum.15 = f32[6,1024]{1,0:T(8,128)S(1)} all-reduce(f32[6,1024]{1,0:T(8,128)S(1)} %pad_maximum_fusion.3), channel_id=1, replica_groups=mesh['dp'=2,'row'=4,'col'=4] {'dp','row','col'}, use_global_device_ids=true, to_apply=%region_7.8 | all-reduce | flops 6144 | bytes 49152 | tf_op jit(solution)/shard_map/psum | solution.py:503
  322.1 2.2 collective-permute-done.17
  324.7 8.0 %collective-permute-done.13 = bf16[256,768]{0,1:T(8,128)(2,1)S(1)} collective-permute-done((bf16[256,768]{0,1:T(8,128)(2,1)S(1)}, bf16[256,768]{0,1:T(8,128)(2,1)S(1)}, u32[]{:S(2)}, u32[]{:S(2)}) %collective-permute-start.13) | collective-permute-done | bytes 393248 | tf_op jit(solution)/shard_map/ppermute | solution.py:381
  332.9 11.0 %collective-permute-done.21 = bf16[256,1024]{1,0:T(8,128)(2,1)S(1)} collective-permute-done((bf16[256,1024]{1,0:T(8,128)(2,1)S(1)}, bf16[256,1024]{1,0:T(8,128)(2,1)S(1)}, u32[]{:S(2)}, u32[]{:S(2)}) %collective-permute-start.21) | collective-permute-done | bytes 524320 | tf_op jit(solution)/shard_map/ppermute | solution.py:381
  344.2 2.5 collective-permute-done.18
  346.8 2.3 collective-permute-start.19
  349.1 8.9 %collective-permute-done.25 = bf16[1024,256]{1,0:T(8,128)(2,1)S(1)} collective-permute-done((bf16[1024,256]{1,0:T(8,128)(2,1)S(1)}, bf16[1024,256]{1,0:T(8,128)(2,1)S(1)}, u32[]{:S(2)}, u32[]{:S(2)}) %collective-permute-start.25) | collective-permute-done | bytes 524320 | tf_op jit(solution)/shard_map/ppermute | solution.py:381
  358.2 8.2 %collective-permute-done.14 = bf16[256,768]{0,1:T(8,128)(2,1)S(1)} collective-permute-done((bf16[256,768]{0,1:T(8,128)(2,1)S(1)}, bf16[256,768]{0,1:T(8,128)(2,1)S(1)}, u32[]{:S(2)}, u32[]{:S(2)}) %collective-permute-start.14) | collective-permute-done | bytes 393248 | tf_op jit(solution)/shard_map/ppermute | solution.py:381
  366.6 2.3 collective-permute-start.15
  368.9 8.8 %collective-permute-done.22 = bf16[256,1024]{1,0:T(8,128)(2,1)S(1)} collective-permute-done((bf16[256,1024]{1,0:T(8,128)(2,1)S(1)}, bf16[256,1024]{1,0:T(8,128)(2,1)S(1)}, u32[]{:S(2)}, u32[]{:S(2)}) %collective-permute-start.22) | collective-permute-done | bytes 524320 | tf_op jit(solution)/shard_map/ppermute | solution.py:381
  377.9 2.3 collective-permute-start.23
  380.9 6.4 %collective-permute-done.26 = bf16[1024,256]{1,0:T(8,128)(2,1)S(1)} collective-permute-done((bf16[1024,256]{1,0:T(8,128)(2,1)S(1)}, bf16[1024,256]{1,0:T(8,128)(2,1)S(1)}, u32[]{:S(2)}, u32[]{:S(2)}) %collective-permute-start.26) | collective-permute-done | bytes 524320 | tf_op jit(solution)/shard_map/ppermute | solution.py:381
  387.5 1.8 collective-permute-start.27
  391.6 8.2 %collective-permute-done.27 = bf16[1024,256]{1,0:T(8,128)(2,1)S(1)} collective-permute-done((bf16[1024,256]{1,0:T(8,128)(2,1)S(1)}, bf16[1024,256]{1,0:T(8,128)(2,1)S(1)}, u32[]{:S(2)}, u32[]{:S(2)}) %collective-permute-start.27) | collective-permute-done | bytes 524320 | tf_op jit(solution)/shard_map/ppermute | solution.py:391
  (172 shorter events, 45.8 us)
Async XLA Ops:
  0.6 8.8 %copy-start.18 = (bf16[256,1024]{1,0:T(8,128)(2,1)S(1)}, bf16[256,1024]{1,0:T(8,128)(2,1)}, u32[]{:S(2)}) copy-start(bf16[256,1024]{1,0:T(8,128)(2,1)} %param.25) | copy-start | bytes 1572868
  1.9 42.4 %collective-permute-start = (bf16[256,768]{0,1:T(8,128)(2,1)S(1)}, bf16[256,768]{0,1:T(8,128)(2,1)}, u32[]{:S(2)}, u32[]{:S(2)}) collective-permute-start(bf16[256,768]{0,1:T(8,128)(2,1)S(1)} %bitcast.62), channel_id=1, source_target_pairs={{0,4},{4,8},{8,12},{12,0},{1,5},{5,9},{9,13},{13,1},{2,6},{6,10},{... | collective-permute-start | bytes 1179656 | tf_op jit(solution)/shard_map/ppermute | solution.py:366
  5.0 14.8 %collective-permute-start.3 = (bf16[256,256]{1,0:T(8,128)(2,1)}, bf16[256,256]{1,0:T(8,128)(2,1)S(1)}, u32[]{:S(2)}, u32[]{:S(2)}) collective-permute-start(bf16[256,256]{1,0:T(8,128)(2,1)} %param.21), channel_id=1, source_target_pairs={{0,4},{4,8},{8,12},{12,0},{1,5},{5,9},{9,13},{13,1},{2,6},{6,10},{... | collective-permute-start | bytes 393224 | tf_op jit(solution)/shard_map/ppermute | solution.py:366
  6.6 39.0 %collective-permute-start.6 = (bf16[256,1024]{1,0:T(8,128)(2,1)}, bf16[256,1024]{1,0:T(8,128)(2,1)}, u32[]{:S(2)}, u32[]{:S(2)}) collective-permute-start(bf16[256,1024]{1,0:T(8,128)(2,1)} %param.25), channel_id=1, source_target_pairs={{0,4},{4,8},{8,12},{12,0},{1,5},{5,9},{9,13},{13,1},{2,6},{6,10},{... | collective-permute-start | bytes 1572872 | tf_op jit(solution)/shard_map/ppermute | solution.py:366
  8.1 39.1 %collective-permute-start.9 = (bf16[1024,256]{1,0:T(8,128)(2,1)}, bf16[1024,256]{1,0:T(8,128)(2,1)}, u32[]{:S(2)}, u32[]{:S(2)}) collective-permute-start(bf16[1024,256]{1,0:T(8,128)(2,1)} %param.27), channel_id=1, source_target_pairs={{0,4},{4,8},{8,12},{12,0},{1,5},{5,9},{9,13},{13,1},{2,6},{6,10},{... | collective-permute-start | bytes 1572872 | tf_op jit(solution)/shard_map/ppermute | solution.py:366
  9.5 10.4 %copy-start.20 = (bf16[256,256]{1,0:T(8,128)(2,1)S(1)}, bf16[256,256]{1,0:T(8,128)(2,1)}, u32[]{:S(2)}) copy-start(bf16[256,256]{1,0:T(8,128)(2,1)} %param.21) | copy-start | bytes 393220
  9.5 10.5 %copy-start.25 = (f32[256]{0:T(256)S(1)}, f32[256]{0:T(256)}, u32[]{:S(2)}) copy-start(f32[256]{0:T(256)} %param.22) | copy-start | bytes 3076
  9.5 10.5 %copy-start.26 = (f32[256]{0:T(256)S(1)}, f32[256]{0:T(256)}, u32[]{:S(2)}) copy-start(f32[256]{0:T(256)} %param.23) | copy-start | bytes 3076
  9.5 10.5 %copy-start.27 = (f32[256]{0:T(256)S(1)}, f32[256]{0:T(256)}, u32[]{:S(2)}) copy-start(f32[256]{0:T(256)} %param.24) | copy-start | bytes 3076
  9.5 10.5 %copy-start.28 = (f32[256]{0:T(256)S(1)}, f32[256]{0:T(256)}, u32[]{:S(2)}) copy-start(f32[256]{0:T(256)} %param.28) | copy-start | bytes 3076
  9.5 10.5 %copy-start.29 = (f32[256]{0:T(256)S(1)}, f32[256]{0:T(256)}, u32[]{:S(2)}) copy-start(f32[256]{0:T(256)} %param.29) | copy-start | bytes 3076
  9.5 10.5 %copy-start.30 = (f32[256]{0:T(256)S(1)}, f32[256]{0:T(256)}, u32[]{:S(2)}) copy-start(f32[256]{0:T(256)} %param.30) | copy-start | bytes 3076
  9.6 10.2 %copy-start.3 = (bf16[1024,1024]{1,0:T(8,128)(2,1)}, bf16[1024,1024]{1,0:T(8,128)(2,1)S(1)}, u32[]{:S(2)}) copy-start(bf16[1024,1024]{1,0:T(8,128)(2,1)S(1)} %constant_dynamic-update-slice_fusion.7) | copy-start | bytes 6291460
  9.9 10.0 %copy-start.6 = (bf16[1024,768]{0,1:T(8,128)(2,1)}, bf16[1024,768]{0,1:T(8,128)(2,1)S(1)}, u32[]{:S(2)}) copy-start(bf16[1024,768]{0,1:T(8,128)(2,1)S(1)} %constant_dynamic-update-slice_fusion.15) | copy-start | bytes 4718596
  19.8 24.4 %collective-permute-start.4 = (bf16[256,256]{1,0:T(8,128)(2,1)S(1)}, bf16[256,256]{1,0:T(8,128)(2,1)S(1)}, u32[]{:S(2)}, u32[]{:S(2)}) collective-permute-start(bf16[256,256]{1,0:T(8,128)(2,1)S(1)} %collective-permute-done.3), channel_id=1, source_target_pairs={{0,4},{4,8},{8,12},{12,0},{1,5},{5,9},{9,13},{13,1},{2,6},{6,10},{... | collective-permute-start | bytes 393224 | tf_op jit(solution)/shard_map/ppermute | solution.py:366
  34.1 18.3 %copy-start.7 = (bf16[1024,768]{0,1:T(8,128)(2,1)S(1)}, bf16[1024,768]{0,1:T(8,128)(2,1)}, u32[]{:S(2)}) copy-start(bf16[1024,768]{0,1:T(8,128)(2,1)} %copy-done.6) | copy-start | bytes 4718596
  44.2 8.2 %collective-permute-start.5 = (bf16[256,256]{1,0:T(8,128)(2,1)S(1)}, bf16[256,256]{1,0:T(8,128)(2,1)S(1)}, u32[]{:S(2)}, u32[]{:S(2)}) collective-permute-start(bf16[256,256]{1,0:T(8,128)(2,1)S(1)} %collective-permute-done.4), channel_id=1, source_target_pairs={{0,4},{4,8},{8,12},{12,0},{1,5},{5,9},{9,13},{13,1},{2,6},{6,10},{... | collective-permute-start | bytes 393224 | tf_op jit(solution)/shard_map/ppermute | solution.py:366
  44.2 16.6 %collective-permute-start.1 = (bf16[256,768]{0,1:T(8,128)(2,1)}, bf16[256,768]{0,1:T(8,128)(2,1)S(1)}, u32[]{:S(2)}, u32[]{:S(2)}) collective-permute-start(bf16[256,768]{0,1:T(8,128)(2,1)} %collective-permute-done), channel_id=1, source_target_pairs={{0,4},{4,8},{8,12},{12,0},{1,5},{5,9},{9,13},{13,1},{2,6},{6,10},{... | collective-permute-start | bytes 1179656 | tf_op jit(solution)/shard_map/ppermute | solution.py:366
  45.6 26.5 %collective-permute-start.7 = (bf16[256,1024]{1,0:T(8,128)(2,1)}, bf16[256,1024]{1,0:T(8,128)(2,1)}, u32[]{:S(2)}, u32[]{:S(2)}) collective-permute-start(bf16[256,1024]{1,0:T(8,128)(2,1)} %collective-permute-done.6), channel_id=1, source_target_pairs={{0,4},{4,8},{8,12},{12,0},{1,5},{5,9},{9,13},{13,1},{2,6},{6,10},{... | collective-permute-start | bytes 1572872 | tf_op jit(solution)/shard_map/ppermute | solution.py:366
  47.2 36.1 %collective-permute-start.10 = (bf16[1024,256]{1,0:T(8,128)(2,1)}, bf16[1024,256]{1,0:T(8,128)(2,1)}, u32[]{:S(2)}, u32[]{:S(2)}) collective-permute-start(bf16[1024,256]{1,0:T(8,128)(2,1)} %collective-permute-done.9), channel_id=1, source_target_pairs={{0,4},{4,8},{8,12},{12,0},{1,5},{5,9},{9,13},{13,1},{2,6},{6,10},{... | collective-permute-start | bytes 1572872 | tf_op jit(solution)/shard_map/ppermute | solution.py:366
  60.8 30.9 %collective-permute-start.2 = (bf16[256,768]{0,1:T(8,128)(2,1)S(1)}, bf16[256,768]{0,1:T(8,128)(2,1)S(1)}, u32[]{:S(2)}, u32[]{:S(2)}) collective-permute-start(bf16[256,768]{0,1:T(8,128)(2,1)S(1)} %collective-permute-done.1), channel_id=1, source_target_pairs={{0,4},{4,8},{8,12},{12,0},{1,5},{5,9},{9,13},{13,1},{2,6},{6,10},{... | collective-permute-start | bytes 1179656 | tf_op jit(solution)/shard_map/ppermute | solution.py:366
  61.9 31.0 %copy-start.16 = (bf16[512,1024]{1,0:T(8,128)(2,1)S(1)}, bf16[512,1024]{1,0:T(8,128)(2,1)}, u32[]{:S(2)}) copy-start(bf16[512,1024]{1,0:T(8,128)(2,1)} %get-tuple-element.79.refs_1_) | copy-start | bytes 3145732
  72.2 53.2 %collective-permute-start.8 = (bf16[256,1024]{1,0:T(8,128)(2,1)}, bf16[256,1024]{1,0:T(8,128)(2,1)}, u32[]{:S(2)}, u32[]{:S(2)}) collective-permute-start(bf16[256,1024]{1,0:T(8,128)(2,1)} %collective-permute-done.7), channel_id=1, source_target_pairs={{0,4},{4,8},{8,12},{12,0},{1,5},{5,9},{9,13},{13,1},{2,6},{6,10},{... | collective-permute-start | bytes 1572872 | tf_op jit(solution)/shard_map/ppermute | solution.py:366
  83.4 48.5 %collective-permute-start.11 = (bf16[1024,256]{1,0:T(8,128)(2,1)}, bf16[1024,256]{1,0:T(8,128)(2,1)}, u32[]{:S(2)}, u32[]{:S(2)}) collective-permute-start(bf16[1024,256]{1,0:T(8,128)(2,1)} %collective-permute-done.10), channel_id=1, source_target_pairs={{0,4},{4,8},{8,12},{12,0},{1,5},{5,9},{9,13},{13,1},{2,6},{6,10},{... | collective-permute-start | bytes 1572872 | tf_op jit(solution)/shard_map/ppermute | solution.py:366
  101.3 26.0 %copy-start.32 = (f32[1024]{0:T(1024)S(1)}, f32[1024]{0:T(1024)}, u32[]{:S(2)}) copy-start(f32[1024]{0:T(1024)} %param.26) | copy-start | bytes 12292
  203.0 9.4 %copy-start.9 = (bf16[1024,768]{0,1:T(8,128)(2,1)S(1)}, bf16[1024,768]{0,1:T(8,128)(2,1)}, u32[]{:S(2)}) copy-start(bf16[1024,768]{0,1:T(8,128)(2,1)} %copy-done.8) | copy-start | bytes 4718596
  243.3 15.8 %copy-start.22 = (f32[8,1024]{1,0:T(8,128)S(1)}, f32[8,1024]{1,0:T(8,128)}, u32[]{:S(2)}) copy-start(f32[8,1024]{1,0:T(8,128)} %get-tuple-element.91) | copy-start | bytes 98308
  243.3 15.8 %copy-start.21 = (f32[8,1024]{1,0:T(8,128)S(1)}, f32[8,1024]{1,0:T(8,128)}, u32[]{:S(2)}) copy-start(f32[8,1024]{1,0:T(8,128)} %get-tuple-element.90) | copy-start | bytes 98308
  257.8 59.0 %collective-permute-start.12 = (bf16[256,768]{0,1:T(8,128)(2,1)}, bf16[256,768]{0,1:T(8,128)(2,1)}, u32[]{:S(2)}, u32[]{:S(2)}) collective-permute-start(bf16[256,768]{0,1:T(8,128)(2,1)} %constant_dynamic-slice_fusion.4), channel_id=1, source_target_pairs={{0,4},{4,8},{8,12},{12,0},{1,5},{5,9},{9,13},{13,1},{2,6},{6,10},{... | collective-permute-start | bytes 1179656 | tf_op jit(solution)/shard_map/ppermute | solution.py:381
  259.0 57.0 %collective-permute-start.16 = (bf16[256,256]{1,0:T(8,128)(2,1)S(1)}, bf16[256,256]{1,0:T(8,128)(2,1)S(1)}, u32[]{:S(2)}, u32[]{:S(2)}) collective-permute-start(bf16[256,256]{1,0:T(8,128)(2,1)S(1)} %constant_dynamic-slice_fusion.3), channel_id=1, source_target_pairs={{0,4},{4,8},{8,12},{12,0},{1,5},{5,9},{9,13},{13,1},{2,6},{6,10},{... | collective-permute-start | bytes 393224 | tf_op jit(solution)/shard_map/ppermute | solution.py:381
  260.0 59.4 %collective-permute-start.20 = (bf16[256,1024]{1,0:T(8,128)(2,1)}, bf16[256,1024]{1,0:T(8,128)(2,1)}, u32[]{:S(2)}, u32[]{:S(2)}) collective-permute-start(bf16[256,1024]{1,0:T(8,128)(2,1)} %constant_dynamic-slice_fusion.2), channel_id=1, source_target_pairs={{0,4},{4,8},{8,12},{12,0},{1,5},{5,9},{9,13},{13,1},{2,6},{6,10},{... | collective-permute-start | bytes 1572872 | tf_op jit(solution)/shard_map/ppermute | solution.py:381
  263.0 61.4 %collective-permute-start.24 = (bf16[1024,256]{1,0:T(8,128)(2,1)}, bf16[1024,256]{1,0:T(8,128)(2,1)S(1)}, u32[]{:S(2)}, u32[]{:S(2)}) collective-permute-start(bf16[1024,256]{1,0:T(8,128)(2,1)} %constant_dynamic-slice_fusion.1), channel_id=1, source_target_pairs={{0,4},{4,8},{8,12},{12,0},{1,5},{5,9},{9,13},{13,1},{2,6},{6,10},{... | collective-permute-start | bytes 1572872 | tf_op jit(solution)/shard_map/ppermute | solution.py:381
  315.3 9.1 %copy-start.5 = (bf16[1024,1024]{1,0:T(8,128)(2,1)S(1)}, bf16[1024,1024]{1,0:T(8,128)(2,1)}, u32[]{:S(2)}) copy-start(bf16[1024,1024]{1,0:T(8,128)(2,1)} %convolution_convert_fusion) | copy-start | bytes 6291460
  316.1 16.7 %copy-start.10 = (bf16[1024,768]{0,1:T(8,128)(2,1)S(1)}, bf16[1024,768]{0,1:T(8,128)(2,1)}, u32[]{:S(2)}) copy-start(bf16[1024,768]{0,1:T(8,128)(2,1)} %convolution_convert_fusion.2) | copy-start | bytes 4718596
  316.1 8.2 %collective-permute-start.17 = (bf16[256,256]{1,0:T(8,128)(2,1)S(1)}, bf16[256,256]{1,0:T(8,128)(2,1)S(1)}, u32[]{:S(2)}, u32[]{:S(2)}) collective-permute-start(bf16[256,256]{1,0:T(8,128)(2,1)S(1)} %add_convert_fusion.11), channel_id=1, source_target_pairs={{0,4},{4,8},{8,12},{12,0},{1,5},{5,9},{9,13},{13,1},{2,6},{6,10},{... | collective-permute-start | bytes 393224 | tf_op jit(solution)/shard_map/ppermute | solution.py:381
  318.0 14.8 %collective-permute-start.13 = (bf16[256,768]{0,1:T(8,128)(2,1)S(1)}, bf16[256,768]{0,1:T(8,128)(2,1)S(1)}, u32[]{:S(2)}, u32[]{:S(2)}) collective-permute-start(bf16[256,768]{0,1:T(8,128)(2,1)S(1)} %add_convert_fusion.8), channel_id=1, source_target_pairs={{0,4},{4,8},{8,12},{12,0},{1,5},{5,9},{9,13},{13,1},{2,6},{6,10},{... | collective-permute-start | bytes 1179656 | tf_op jit(solution)/shard_map/ppermute | solution.py:381
  320.6 23.3 %collective-permute-start.21 = (bf16[256,1024]{1,0:T(8,128)(2,1)S(1)}, bf16[256,1024]{1,0:T(8,128)(2,1)S(1)}, u32[]{:S(2)}, u32[]{:S(2)}) collective-permute-start(bf16[256,1024]{1,0:T(8,128)(2,1)S(1)} %add_convert_fusion.5), channel_id=1, source_target_pairs={{0,4},{4,8},{8,12},{12,0},{1,5},{5,9},{9,13},{13,1},{2,6},{6,10},{... | collective-permute-start | bytes 1572872 | tf_op jit(solution)/shard_map/ppermute | solution.py:381
  324.3 22.4 %collective-permute-start.18 = (bf16[256,256]{1,0:T(8,128)(2,1)S(1)}, bf16[256,256]{1,0:T(8,128)(2,1)S(1)}, u32[]{:S(2)}, u32[]{:S(2)}) collective-permute-start(bf16[256,256]{1,0:T(8,128)(2,1)S(1)} %add_convert_fusion.10), channel_id=1, source_target_pairs={{0,4},{4,8},{8,12},{12,0},{1,5},{5,9},{9,13},{13,1},{2,6},{6,10},{... | collective-permute-start | bytes 393224 | tf_op jit(solution)/shard_map/ppermute | solution.py:381
  324.6 33.4 %collective-permute-start.25 = (bf16[1024,256]{1,0:T(8,128)(2,1)S(1)}, bf16[1024,256]{1,0:T(8,128)(2,1)S(1)}, u32[]{:S(2)}, u32[]{:S(2)}) collective-permute-start(bf16[1024,256]{1,0:T(8,128)(2,1)S(1)} %add_convert_fusion.2), channel_id=1, source_target_pairs={{0,4},{4,8},{8,12},{12,0},{1,5},{5,9},{9,13},{13,1},{2,6},{6,10},{... | collective-permute-start | bytes 1572872 | tf_op jit(solution)/shard_map/ppermute | solution.py:381
  332.9 33.6 %collective-permute-start.14 = (bf16[256,768]{0,1:T(8,128)(2,1)S(1)}, bf16[256,768]{0,1:T(8,128)(2,1)S(1)}, u32[]{:S(2)}, u32[]{:S(2)}) collective-permute-start(bf16[256,768]{0,1:T(8,128)(2,1)S(1)} %add_convert_fusion.7), channel_id=1, source_target_pairs={{0,4},{4,8},{8,12},{12,0},{1,5},{5,9},{9,13},{13,1},{2,6},{6,10},{... | collective-permute-start | bytes 1179656 | tf_op jit(solution)/shard_map/ppermute | solution.py:381
  344.2 33.5 %collective-permute-start.22 = (bf16[256,1024]{1,0:T(8,128)(2,1)S(1)}, bf16[256,1024]{1,0:T(8,128)(2,1)S(1)}, u32[]{:S(2)}, u32[]{:S(2)}) collective-permute-start(bf16[256,1024]{1,0:T(8,128)(2,1)S(1)} %add_convert_fusion.4), channel_id=1, source_target_pairs={{0,4},{4,8},{8,12},{12,0},{1,5},{5,9},{9,13},{13,1},{2,6},{6,10},{... | collective-permute-start | bytes 1572872 | tf_op jit(solution)/shard_map/ppermute | solution.py:381
  346.8 33.4 %collective-permute-start.19 = (bf16[256,256]{1,0:T(8,128)(2,1)S(1)}, bf16[256,256]{1,0:T(8,128)(2,1)S(1)}, u32[]{:S(2)}, u32[]{:S(2)}) collective-permute-start(bf16[256,256]{1,0:T(8,128)(2,1)S(1)} %add_convert_fusion.9), channel_id=1, source_target_pairs={{0,16},{16,0},{1,17},{17,1},{2,18},{18,2},{3,19},{19,3},{4,20},{20... | collective-permute-start | bytes 393224 | tf_op jit(solution)/shard_map/ppermute | solution.py:391
  358.2 29.1 %collective-permute-start.26 = (bf16[1024,256]{1,0:T(8,128)(2,1)S(1)}, bf16[1024,256]{1,0:T(8,128)(2,1)S(1)}, u32[]{:S(2)}, u32[]{:S(2)}) collective-permute-start(bf16[1024,256]{1,0:T(8,128)(2,1)S(1)} %add_convert_fusion.1), channel_id=1, source_target_pairs={{0,4},{4,8},{8,12},{12,0},{1,5},{5,9},{9,13},{13,1},{2,6},{6,10},{... | collective-permute-start | bytes 1572872 | tf_op jit(solution)/shard_map/ppermute | solution.py:381
  366.6 22.7 %collective-permute-start.15 = (bf16[256,768]{0,1:T(8,128)(2,1)S(1)}, bf16[256,768]{0,1:T(8,128)(2,1)S(1)}, u32[]{:S(2)}, u32[]{:S(2)}) collective-permute-start(bf16[256,768]{0,1:T(8,128)(2,1)S(1)} %add_convert_fusion.6), channel_id=1, source_target_pairs={{0,16},{16,0},{1,17},{17,1},{2,18},{18,2},{3,19},{19,3},{4,20},{20... | collective-permute-start | bytes 1179656 | tf_op jit(solution)/shard_map/ppermute | solution.py:391
  377.9 12.6 %collective-permute-start.23 = (bf16[256,1024]{1,0:T(8,128)(2,1)S(1)}, bf16[256,1024]{1,0:T(8,128)(2,1)S(1)}, u32[]{:S(2)}, u32[]{:S(2)}) collective-permute-start(bf16[256,1024]{1,0:T(8,128)(2,1)S(1)} %add_convert_fusion.3), channel_id=1, source_target_pairs={{0,16},{16,0},{1,17},{17,1},{2,18},{18,2},{3,19},{19,3},{4,20},{20... | collective-permute-start | bytes 1572872 | tf_op jit(solution)/shard_map/ppermute | solution.py:391
  387.5 12.4 %collective-permute-start.27 = (bf16[1024,256]{1,0:T(8,128)(2,1)S(1)}, bf16[1024,256]{1,0:T(8,128)(2,1)S(1)}, u32[]{:S(2)}, u32[]{:S(2)}) collective-permute-start(bf16[1024,256]{1,0:T(8,128)(2,1)S(1)} %add_convert_fusion), channel_id=1, source_target_pairs={{0,16},{16,0},{1,17},{17,1},{2,18},{18,2},{3,19},{19,3},{4,20},{20... | collective-permute-start | bytes 1572872 | tf_op jit(solution)/shard_map/ppermute | solution.py:391
  390.5 10.5 %copy-start.19 = (bf16[512,256]{1,0:T(8,128)(2,1)S(1)}, bf16[512,256]{1,0:T(8,128)(2,1)}, u32[]{:S(2)}) copy-start(bf16[512,256]{1,0:T(8,128)(2,1)} %get-tuple-element.161) | copy-start | bytes 786436
  390.5 11.2 %copy-start.2 = (f32[512,256]{1,0:T(8,128)S(1)}, f32[512,256]{1,0:T(8,128)}, u32[]{:S(2)}) copy-start(f32[512,256]{1,0:T(8,128)} %shard_map.275) | copy-start | bytes 1572868
  (18 other events, 49.6 us)

commit v2 on v1

--- a/solution.py
+++ b/solution.py
@@ -6,6 +6,7 @@
 from jax.experimental import pallas as pl
 from jax.experimental.pallas import tpu as pltpu
 from jax.sharding import PartitionSpec as P
+
 
 HD = 64
 
@@ -71,30 +72,111 @@
     )
 
 
-def place(count):
+def place():
     me = lax.axis_index("col")
     chip, core = lax.div(me, 2), lax.rem(me, 2)
     return me, chip, core, chip * 2 + 1 - core
 
 
-def greet(count, me):
+def greet(count, me, rows_n=1, dp_n=1):
     barrier = pltpu.get_barrier_semaphore()
-    for step in range(1, count):
-        pl.semaphore_signal(
-            barrier,
-            inc=1,
-            device_id={"col": lax.rem(me + step, count)},
-            device_id_type=MESH,
-        )
-    pl.semaphore_wait(barrier, count - 1)
+    targets = [{"col": lax.rem(me + step, count)} for step in range(1, count)]
+    if rows_n > 1:
+        row = lax.axis_index("row")
+        targets.append({"row": lax.rem(row + 1, rows_n)})
+        targets.append({"row": lax.rem(row + rows_n - 1, rows_n)})
+        dp = lax.axis_index("dp")
+        targets += [{"dp": lax.rem(dp + step, dp_n)} for step in range(1, dp_n)]
+    for target in targets:
+        pl.semaphore_signal(barrier, inc=1, device_id=target, device_id_type=MESH)
+    pl.semaphore_wait(barrier, len(targets))
 
 
 def rows_of(index, size):
     return pl.ds(pl.multiple_of(index * size, size), size)
 
 
+def row_view(axis, shape, dp_n):
+    share = shape[0] // dp_n
+    if axis == 0:
+        return lambda ref, index, part: ref.at[
+            pl.ds(pl.multiple_of(index * shape[0] + part * share, share), share), :
+        ]
+    if shape[1] % 128 == 0:
+        return lambda ref, index, part: ref.at[
+            pl.ds(pl.multiple_of(part * share, share), share), rows_of(index, shape[1])
+        ]
+    return lambda ref, index, part: ref.at[
+        index, pl.ds(pl.multiple_of(part * share, share), share), :
+    ]
+
+
+def full_shape(axis, shape, rows_n):
+    if axis == 0:
+        return (shape[0] * rows_n, shape[1])
+    if shape[1] % 128 == 0:
+        return (shape[0], shape[1] * rows_n)
+    return (rows_n,) + tuple(shape)
+
+
+def unstack(whole):
+    if whole.ndim == 2:
+        return whole
+    return jnp.moveaxis(whole, 0, 1).reshape(whole.shape[1], -1)
+
+
+def weight_ring(rows_n, dp_n, block, whole, axis, sems):
+    zs, zr, xs, xr = sems
+    row, dp = lax.axis_index("row"), lax.axis_index("dp")
+    view = row_view(axis, block.shape, dp_n)
+    share = block.shape[0] // dp_n
+    after = lax.rem(row + 1, rows_n)
+    started = []
+
+    def start(src, dst, send, recv, target):
+        copy = pltpu.make_async_remote_copy(
+            src_ref=src, dst_ref=dst, send_sem=send, recv_sem=recv,
+            device_id=target, device_id_type=MESH,
+        )
+        copy.start()
+        started.append(copy)
+        return copy
+
+    source = block.at[pl.ds(pl.multiple_of(dp * share, share), share), :]
+    moving = start(source, view(whole, row, dp), zs.at[0], zr.at[0], {"row": after})
+    for part in range(dp_n):
+        view(whole, row, part)[...] = block[pl.ds(part * share, share), :]
+    swaps = []
+    yield
+    for step in range(rows_n - 1):
+        moving.wait_recv()
+        here = view(whole, lax.rem(row - 1 - step + rows_n, rows_n), dp)
+        if step < rows_n - 2:
+            moving = start(here, here, zs.at[step + 1], zr.at[step + 1], {"row": after})
+        for other in range(1, dp_n):
+            slot = step * dp_n + other
+            swaps.append(
+                start(here, here, xs.at[slot], xr.at[slot], {"dp": lax.rem(dp + other, dp_n)})
+            )
+        yield
+    for copy in swaps:
+        copy.wait_recv()
+    for copy in started:
+        copy.wait_send()
+
+
+def ring_sems(rows_n, dp_n):
+    dma = pltpu.SemaphoreType.DMA
+    return [dma((rows_n,)), dma((rows_n,)), dma((rows_n * dp_n,)), dma((rows_n * dp_n,))]
+
+
+def advance(rings):
+    for ring in rings:
+        next(ring, None)
+
+
 def start_reduce(count, view, slots, sums, s1, r1, s2, r2):
-    me, chip, core, partner = place(count)
+    _, chip, core, partner = place()
     chips = count // 2
     far = lambda step: lax.rem(chip + step, chips)
     order = list(range(1, chips)) + [0]
@@ -132,8 +214,8 @@
     return total
 
 
-def gather_blocks(count, source, view, s3, r3, s4, r4):
-    me, chip, core, partner = place(count)
+def gather_blocks(count, source, view, s3, r3):
+    me, chip, core, partner = place()
     chips = count // 2
     sent = []
     for step in range(1, chips):
@@ -146,7 +228,7 @@
 
 
 def gather_rest(count, view, pending, s4, r4):
-    me, chip, core, partner = place(count)
+    _, chip, core, partner = place()
     chips = count // 2
     sent, near = pending
     passed = []
@@ -162,14 +244,25 @@
         copy.wait_send()
 
 
-def spread_kernel(count, x_ref, og_ref, par_ref, full_ref, og_out, par_out, *sems):
-    s3, r3, s4, r4, sa, ra, sb, rb = sems
+def spread_kernel(count, rows_n, dp_n, axes, *refs):
+    n = len(axes)
+    x_ref, og_ref, par_ref = refs[:3]
+    blocks = refs[3 : 3 + n]
+    full_ref, og_out, par_out = refs[3 + n : 6 + n]
+    wholes = refs[6 + n : 6 + 2 * n]
+    sems = refs[6 + 2 * n :]
+    s3, r3, s4, r4, sa, ra, sb, rb = sems[:8]
     me = lax.axis_index("col")
     width = x_ref.shape[1]
     rows = og_ref.shape[0] // count
-    greet(count, me)
+    greet(count, me, rows_n, dp_n)
+    rings = [
+        weight_ring(rows_n, dp_n, blocks[i], wholes[i], axes[i], sems[8 + 4 * i : 12 + 4 * i])
+        for i in range(n)
+    ]
+    advance(rings)
     view = lambda index: full_ref.at[:, rows_of(index, width)]
-    pending = gather_blocks(count, x_ref, view, s3, r3, s4, r4)
+    pending = gather_blocks(count, x_ref, view, s3, r3)
     mine = rows_of(me, width)
     others = []
     for step in range(1, count):
@@ -183,44 +276,64 @@
     full_ref[:, mine] = x_ref[...]
     og_out[:, mine] = og_ref[rows_of(me, rows), :]
     par_out[:, mine] = par_ref[...]
+    advance(rings)
     gather_rest(count, view, pending, s4, r4)
+    for _ in range(rows_n):
+        advance(rings)
     for copy in others:
         copy.wait()
 
 
-def spread_all(count, x, og, par):
+def spread_all(count, rows_n, dp_n, x, og, par, blocks, axes):
     tokens, width = x.shape
     dma = pltpu.SemaphoreType.DMA
     return pl.pallas_call(
-        functools.partial(spread_kernel, count),
+        functools.partial(spread_kernel, count, rows_n, dp_n, axes),
         out_shape=(
             jax.ShapeDtypeStruct((tokens, width * count), x.dtype),
             jax.ShapeDtypeStruct((tokens // count, width * count), og.dtype),
             jax.ShapeDtypeStruct((par.shape[0], width * count), par.dtype),
+        )
+        + tuple(
+            jax.ShapeDtypeStruct(full_shape(axis, block.shape, rows_n), block.dtype)
+            for axis, block in zip(axes, blocks)
         ),
-        in_specs=[VMEM] * 3,
-        out_specs=(VMEM,) * 3,
-        scratch_shapes=[dma((count,))] * 8,
+        in_specs=[VMEM] * (3 + len(blocks)),
+        out_specs=(VMEM,) * (3 + len(blocks)),
+        scratch_shapes=[dma((count,))] * 8 + ring_sems(rows_n, dp_n) * len(blocks),
         compiler_params=pltpu.CompilerParams(collective_id=0, has_side_effects=True),
         cost_estimate=COST,
-    )(x, og, par)
-
-
-def middle_kernel(count, mid, n_aux, n_out, exchange, *refs):
+    )(x, og, par, *blocks)
+
+
+def middle_kernel(count, mid, n_aux, n_out, exchange, ring_of, *refs):
     part = refs[0]
+    rings = []
+    if ring_of is not None:
+        rows_n, dp_n, axis = ring_of
+        n_aux, n_out = n_aux + 1, n_out + 1
     aux = refs[1 : 1 + n_aux]
     full = refs[1 + n_aux]
     outs = refs[2 + n_aux : 2 + n_aux + n_out]
-    slots, sums, swap, s1, r1, s2, r2, s3, r3, s4, r4, sa, ra = refs[2 + n_aux + n_out :]
+    slots, sums, swap, s1, r1, s2, r2, s3, r3, s4, r4, sa, ra = refs[2 + n_aux + n_out :][:13]
     me = lax.axis_index("col")
     rows = part.shape[0] // count
-    greet(count, me)
+    if ring_of is None:
+        greet(count, me)
+    else:
+        greet(count, me, rows_n, dp_n)
+        rings.append(
+            weight_ring(rows_n, dp_n, aux[-1], outs[-1], axis, refs[2 + n_aux + n_out :][13:])
+        )
+        aux, outs = aux[:-1], outs[:-1]
+    advance(rings)
     view = lambda index: part.at[rows_of(index, rows), :]
     pending = start_reduce(count, view, slots, sums, s1, r1, s2, r2)
+    advance(rings)
     total = finish_reduce(count, view, slots, sums, pending)
     mid(total, me, aux, outs, full.at[rows_of(me, rows), :], swap)
     out_view = lambda index: full.at[rows_of(index, rows), :]
-    pending = gather_blocks(count, out_view(me), out_view, s3, r3, s4, r4)
+    pending = gather_blocks(count, out_view(me), out_view, s3, r3)
     others = []
     if exchange:
         laid = outs[0]
@@ -238,17 +351,36 @@
             )
             others[-1].start()
         laid[rows_of(me, rows), :] = swap[:, rows_of(me, width)]
+    advance(rings)
     gather_rest(count, out_view, pending, s4, r4)
+    if rings:
+        for _ in range(rows_n):
+            advance(rings)
     for copy in others:
         copy.wait()
 
 
-def middle(count, part, aux, mid, outs, exchange, cid):
+def middle(count, part, aux, mid, outs, exchange, cid, ring_of=None, block=None):
+    body = functools.partial(
+        middle_kernel, count, mid, len(aux), len(outs), exchange, ring_of
+    )
+    extra = []
+    if ring_of is not None:
+        rows_n, dp_n, axis = ring_of
+        aux = tuple(aux) + (block,)
+        outs = tuple(outs) + (
+            jax.ShapeDtypeStruct(full_shape(axis, block.shape, rows_n), block.dtype),
+        )
+        extra = ring_sems(rows_n, dp_n)
     tokens, width = part.shape
     rows = tokens // count
     dma = pltpu.SemaphoreType.DMA
+    return middle_call(body, tokens, width, outs, aux, count, rows, dma, extra, cid, part)
+
+
+def middle_call(body, tokens, width, outs, aux, count, rows, dma, extra, cid, part):
     return pl.pallas_call(
-        functools.partial(middle_kernel, count, mid, len(aux), len(outs), exchange),
+        body,
         out_shape=(jax.ShapeDtypeStruct((tokens, width), jnp.bfloat16),) + tuple(outs),
         in_specs=[VMEM] * (1 + len(aux)),
         out_specs=(VMEM,) * (1 + len(outs)),
@@ -257,39 +389,109 @@
             pltpu.VMEM((count, rows, width), jnp.bfloat16),
             pltpu.VMEM((rows, width), jnp.bfloat16),
         ]
-        + [dma((count,))] * 10,
+        + [dma((count,))] * 10
+        + extra,
         compiler_params=pltpu.CompilerParams(collective_id=cid, has_side_effects=True),
         cost_estimate=COST,
     )(part, *aux)
 
 
-def last_kernel(count, part, back_full, out, slots, sums, s1, r1, s2, r2):
+def last_kernel(count, rows_n, dp_n, *refs):
+    part, back_full, six_two, six_one, local, out, sums_out = refs[:7]
+    slots, sums, gathered, packed, landed = refs[7:12]
+    s1, r1, s2, r2, sa, ra, sb, rb = refs[12:]
     me = lax.axis_index("col")
     width = part.shape[1] // count
-    greet(count, me)
+    row, dp = lax.axis_index("row"), lax.axis_index("dp")
+    peers = rows_n * dp_n
+    mine = dp * rows_n + row
+    barrier = pltpu.get_barrier_semaphore()
+
+    def peer(step):
+        index = lax.rem(mine + step, peers)
+        return {"dp": lax.div(index, rows_n), "row": lax.rem(index, rows_n)}
+
+    for step in range(1, count):
+        target = {"col": lax.rem(me + step, count)}
+        pl.semaphore_signal(barrier, inc=1, device_id=target, device_id_type=MESH)
+    for step in range(1, peers):
+        pl.semaphore_signal(barrier, inc=1, device_id=peer(step), device_id_type=MESH)
+    pl.semaphore_wait(barrier, count + peers - 2)
     view = lambda index: part.at[:, rows_of(index, width)]
+    small = []
+    for step in range(1, count):
+        target = lax.rem(me + step, count)
+        for which, ref in enumerate((six_two, six_one)):
+            small.append(
+                remote(
+                    ref.at[:, rows_of(target, width)],
+                    gathered.at[step, which],
+                    sa.at[2 * step + which],
+                    ra.at[2 * step + which],
+                    target,
+                )
+            )
+            small[-1].start()
     pending = start_reduce(count, view, slots, sums, s1, r1, s2, r2)
+    for copy in small:
+        copy.wait()
+    for which, ref in enumerate((six_two, six_one)):
+        total = ref[:, rows_of(me, width)]
+        for step in range(1, count):
+            total = total + gathered[step, which]
+        packed[pl.ds(8 * which, 8), :] = total
+    packed[pl.ds(16, local.shape[0]), :] = local[...]
+    sent = []
+    for step in range(1, peers):
+        sent.append(
+            pltpu.make_async_remote_copy(
+                src_ref=packed,
+                dst_ref=landed.at[mine],
+                send_sem=sb.at[step],
+                recv_sem=rb.at[step],
+                device_id=peer(step),
+                device_id_type=MESH,
+            )
+        )
+        sent[-1].start()
+    landed[mine] = packed[...]
     total = finish_reduce(count, view, slots, sums, pending)
     out[...] = total + back_full[:, rows_of(me, width)].astype(jnp.float32)
-
-
-def last(count, part, back_full):
+    for copy in sent:
+        copy.wait()
+    total = landed[0]
+    for index in range(1, peers):
+        total = total + landed[index]
+    sums_out[...] = total
+
+
+def last(count, rows_n, dp_n, part, back_full, six_two, six_one, local):
     tokens, width = part.shape
     cols = width // count
     dma = pltpu.SemaphoreType.DMA
+    height = 16 + local.shape[0]
+    peers = rows_n * dp_n
     return pl.pallas_call(
-        functools.partial(last_kernel, count),
-        out_shape=jax.ShapeDtypeStruct((tokens, cols), jnp.float32),
-        in_specs=[VMEM] * 2,
-        out_specs=VMEM,
+        functools.partial(last_kernel, count, rows_n, dp_n),
+        out_shape=(
+            jax.ShapeDtypeStruct((tokens, cols), jnp.float32),
+            jax.ShapeDtypeStruct((height, cols), jnp.float32),
+        ),
+        in_specs=[VMEM] * 5,
+        out_specs=(VMEM,) * 2,
         scratch_shapes=[
             pltpu.VMEM((count // 2, tokens, cols), jnp.bfloat16),
             pltpu.VMEM((count, tokens, cols), jnp.bfloat16),
+            pltpu.VMEM((count, 2, 8, cols), jnp.float32),
+            pltpu.VMEM((height, cols), jnp.float32),
+            pltpu.VMEM((peers, height, cols), jnp.float32),
         ]
-        + [dma((count,))] * 4,
+        + [dma((count,))] * 4
+        + [dma((2 * count,))] * 2
+        + [dma((peers,))] * 2,
         compiler_params=pltpu.CompilerParams(collective_id=4, has_side_effects=True),
         cost_estimate=COST,
-    )(part, back_full)
+    )(part, back_full, six_two, six_one, local)
 
 
 def norm_parts(total):
@@ -325,7 +527,7 @@
 
 def mid_two(total, me, aux, outs, block, swap):
     act, grad, par = aux
-    laid, back_out, sum_out = outs
+    _, back_out, sum_out = outs
     total = act[...] + (total + par[3:4, :])
     normed, inverse = norm_parts(total)
     gain = par[4:5, :]
@@ -333,6 +535,7 @@
     top = grad[...].astype(jnp.float32)
     back = norm_back(top, normed, inverse, gain)
     back_out[...] = back
+    sum_out[...] = jnp.zeros(sum_out.shape, jnp.float32)
     sum_out[0:1, :] = column_sum(top * normed)
     sum_out[1:2, :] = column_sum(top)
     sum_out[2:3, :] = column_sum(back)
@@ -345,26 +548,11 @@
     upstream = back_two[...] + total
     normed = normed_ref[...]
     back = norm_back(upstream, normed, inverse[:, 0:1], par[1:2, :])
+    sum_out[...] = jnp.zeros(sum_out.shape, jnp.float32)
     sum_out[0:1, :] = column_sum(upstream * normed)
     sum_out[1:2, :] = column_sum(upstream)
     sum_out[2:3, :] = column_sum(back)
     block[...] = back.astype(jnp.bfloat16)
-
-
-def ring_gather(block, axis, count):
-    me = lax.axis_index("row")
-    ring = [(i, (i + 1) % count) for i in range(count)]
-    size = block.shape[axis]
-    shape = list(block.shape)
-    shape[axis] = size * count
-    whole = jnp.zeros(shape, block.dtype)
-    for step in range(count):
-        whole = lax.dynamic_update_slice_in_dim(
-            whole, block, lax.rem(me - step + count, count) * size, axis
-        )
-        if step < count - 1:
-            block = lax.ppermute(block, "row", ring)
-    return whole
 
 
 def ring_scatter(part, axis, count):
@@ -423,15 +611,21 @@
     head_shape = (seq_count, seq_len, head_count, HD)
     width = col_width * cols_n
     part_rows = tokens_dev // cols_n
-    qkv_full = ring_gather(w_qkv.reshape(w_qkv.shape[0], -1), 0, rows_n)
-    out_full = ring_gather(w_out, 1, rows_n)
-    up_full = ring_gather(w_up, 0, rows_n)
-    down_full = ring_gather(w_down, 1, rows_n)
     blank = jnp.zeros_like(out_bias)
     par = jnp.stack(
         [out_bias, norm_gain, norm_shift, down_bias, final_gain, final_shift, blank, blank]
     )
-    x_full, top_rows, par_full = spread_all(cols_n, hidden_in, out_grad, par)
+    x_full, top_rows, par_full, qkv_full, out_full, up_full = spread_all(
+        cols_n,
+        rows_n,
+        dp_n,
+        hidden_in,
+        out_grad,
+        par,
+        (w_qkv.reshape(w_qkv.shape[0], -1), w_out, w_up),
+        (0, 1, 0),
+    )
+    out_full = unstack(out_full)
     projected = jnp.dot(x_full, qkv_full, preferred_element_type=f32)
     query = (projected[:, :col_width] + query_bias).astype(bf16).reshape(head_shape)
     keys = projected[:, col_width : 2 * col_width].astype(bf16).reshape(head_shape)
@@ -440,7 +634,7 @@
     ctx_rows = context.reshape(tokens_dev, col_width)
     block_f32 = jax.ShapeDtypeStruct((part_rows, width), f32)
     sums_f32 = jax.ShapeDtypeStruct((8, width), f32)
-    attn_full, attn_act, normed_one, inverse_one = middle(
+    attn_full, attn_act, normed_one, inverse_one, down_full = middle(
         cols_n,
         jnp.dot(ctx_rows, out_full, preferred_element_type=f32).astype(bf16),
         (x_full, par_full),
@@ -448,7 +642,10 @@
         (block_f32, block_f32, jax.ShapeDtypeStruct((part_rows, 128), f32)),
         False,
         1,
-    )
+        (rows_n, dp_n, 1),
+        w_down,
+    )
+    down_full = unstack(down_full)
     up_pre = jnp.dot(attn_full, up_full, preferred_element_type=f32) + up_bias
     act_f, slope = gelu_parts(up_pre)
     act = act_f.astype(bf16)
@@ -479,11 +676,8 @@
     ubias_part = jnp.sum(up_back, axis=0)
     wout_part = jnp.dot(ctx_rows.T, back_one_full, preferred_element_type=f32).astype(bf16)
     wout_grad = pair_sum(ring_scatter(wout_part, 1, rows_n), dp_n)
-    ctx_back = (
-        jnp.dot(back_one_full, out_full.T, preferred_element_type=f32)
-        .astype(bf16)
-        .reshape(head_shape)
-    )
+    ctx_back = jnp.dot(back_one_full, out_full.T, preferred_element_type=f32).astype(bf16)
+    ctx_back = ctx_back.reshape(head_shape)
     q_back, k_back, v_back = lax.map(
         attend_back, (query, keys, values, doc_ids, ctx_back, log_total)
     )
@@ -495,31 +689,31 @@
     qkv_back = jnp.concatenate([q_back.astype(bf16), k_back.astype(bf16), v_back.astype(bf16)], axis=1)
     wqkv_part = jnp.dot(x_full.T, qkv_back, preferred_element_type=f32).astype(bf16)
     wqkv_grad = pair_sum(ring_scatter(wqkv_part, 0, rows_n), dp_n).reshape(w_qkv.shape)
-    hidden_grad = last(
-        cols_n,
-        jnp.dot(qkv_back, qkv_full.T, preferred_element_type=f32).astype(bf16),
-        back_one_full,
-    )
-    six = lax.psum(jnp.concatenate([sums_two[:3], sums_one[:3]], axis=0), ("dp", "row", "col"))
-    six = lax.dynamic_slice_in_dim(six, lax.axis_index("col") * col_width, col_width, 1)
-    local = lax.psum(jnp.concatenate([ubias_part, qbias_part, vbias_part]), ("dp", "row"))
+    local = jnp.concatenate([ubias_part, qbias_part, vbias_part])
+    filled = -(-local.shape[0] // (8 * col_width)) * 8 * col_width
+    local = jnp.pad(local, (0, filled - local.shape[0])).reshape(-1, col_width)
+    hidden_part = jnp.dot(qkv_back, qkv_full.T, preferred_element_type=f32).astype(bf16)
+    hidden_grad, sums = last(
+        cols_n, rows_n, dp_n, hidden_part, back_one_full, sums_two, sums_one, local
+    )
+    local = sums[16:].reshape(-1)
     hidden_w = ubias_part.shape[0]
     return (
         layer_out,
         hidden_grad,
         wqkv_grad,
         local[hidden_w : hidden_w + col_width],
-        local[hidden_w + col_width :],
+        local[hidden_w + col_width : hidden_w + 2 * col_width],
         wout_grad,
-        six[5],
-        six[3],
-        six[4],
+        sums[10],
+        sums[8],
+        sums[9],
         wup_grad,
         local[:hidden_w],
         wdown_grad,
-        six[2],
-        six[0],
-        six[1],
+        sums[2],
+        sums[0],
+        sums[1],
     )
 
 

time: 403 us -> 320 us (0.79)
  blocking collectives: 68.1 us -> 0 us
  Pallas kernels: 93.9 us -> 159 us
  waiting for transfers between devices: 118 us -> 66.4 us
  local copies, waits for them, and re-layouts: 28.9 us -> 14.8 us
  starting transfers between devices: 28.9 us -> 15.8 us
    psum x2 -> x0, blocking collectives: 68.1 us -> none  [the longest x1 49.8 us: per_device(): lax.psum(jnp.concatenate([sums_two[:3], sums_one[:3]], axis=0), ('dp', 'r...]
    pallas_call x5, Pallas kernels: 93.9 us -> 159 us  [the longest x3 76.1 us: middle_call(): pl.pallas_call(body, out_shape=(jax.ShapeDtypeStruct((tokens, width), jnp...]
    ppermute x12 -> x0, waiting for transfers between devices: 53.8 us -> none  [ring_gather(): block = lax.ppermute(block, 'row', ring)]
    dynamic_update_slice x16 -> x0, local copies, waits for them, and re-layouts: 11.8 us -> none  [ring_gather(): lax.dynamic_update_slice_in_dim(whole, block, lax.rem(me - step + count,...]
    ppermute x12 -> x0, starting transfers between devices: 11.4 us -> none  [ring_gather(): block = lax.ppermute(block, 'row', ring)]
  transfers between devices with their start and end apart: 28 -> 16, of which waited for: 16 -> 9; matrix products, arithmetic and copies ran while one was open for 9% -> 6% of each run, Pallas kernels for 9% -> 9%
where the time goes in v2:
time: 320 us; the launch traced here: 319 us
  Pallas kernels  159 us (50%)
  waiting for transfers between devices  66.4 us (21%)
  matrix products  51.1 us (16%)
  starting transfers between devices  15.8 us (5%)
  local copies, waits for them, and re-layouts  14.8 us (5%)
  other arithmetic  10.8 us (3%)
    pallas_call x3, Pallas kernels, middle_call(): pl.pallas_call(body, out_shape=(jax.ShapeDtypeStruct((tokens, width), jnp...  76.1 us
    ppermute x12, waiting for transfers between devices, ring_scatter(): moved = lax.ppermute(total, 'row', ring)  58.2 us
    pallas_call x1, Pallas kernels, spread_all(): pl.pallas_call(functools.partial(spread_kernel, count, rows_n, dp_n, axes...  53.5 us
    pallas_call x1, Pallas kernels, last(): pl.pallas_call(functools.partial(last_kernel, count, rows_n, dp_n), out_s...  29.7 us
    ppermute x12, starting transfers between devices, ring_scatter(): moved = lax.ppermute(total, 'row', ring)  9.57 us
    dot_general x1, matrix products, attend_back(): jnp.einsum('hqk,khd->qhd', score_back, keys, preferred_element_type=jnp.f...  8.81 us
    ppermute x4, waiting for transfers between devices, pair_sum(): return result + lax.ppermute(moved, 'dp', ring).astype(jnp.float32)  8.14 us
    dot_general x1, matrix products, attend_back(): jnp.einsum('hqk,qhd->khd', score_back, query, preferred_element_type=jnp....  7.38 us
  transfers between devices with their start and end apart: 16, of which 9 were waited for; matrix products, arithmetic and copies ran while one was open for 6% of the time, Pallas kernels for 9%

profile of v2, /device:TPU:0, one launch (start us, length us, event | category | flops | bytes accessed | tf_op | source)
XLA Modules:
  0.0 319.4 jit_solution(13346166175497956982)
XLA Ops:
  0.6 1.2 copy.43
  2.7 1.4 stack.31.refs_2_
  4.1 53.5 %shard_map.271 = (bf16[512,1024]{1,0:T(8,128)(2,1)}, bf16[128,1024]{1,0:T(8,128)(2,1)}, f32[8,1024]{1,0:T(8,128)}, bf16[1024,768]{1,0:T(8,128)(2,1)}, bf16[256,1...) custom-call(bf16[512,256]{1,0:T(8,128)(2,1)} %refs_0_.1, bf16[512,256]{1,0:T(8,128)(2,1)} %refs_1_.1, ...), custom_call_target="tpu_custom_call" | custom-call | bytes 30000000 | tf_op jit(solution)/shard_map/pallas_call | solution.py:290
  57.7 2.7 fusion.42
  63.4 1.0 copy-done
  64.5 1.2 convolution_convert_fusion.9
  65.7 1.4 convolution_convert_fusion.6.refs_0_
  67.2 31.1 %shard_map.272 = (bf16[512,1024]{1,0:T(8,128)(2,1)}, f32[128,1024]{1,0:T(8,128)}, f32[128,1024]{1,0:T(8,128)}, f32[128,128]{1,0:T(8,128)}, bf16[1024,1024]{1,0:T(8,128)(2,1)}) custom-call(bf16[512,1024]{1,0:T(8,128)(2,1)} %convolution_convert_fusion.6.refs_0_, bf16[512,1024]{1,0:T(8,128)(2,1)} %get-tuple-element.85.refs_1_, ...), custom_call_target="tpu_custom_call" | custom-call | bytes 30000000 | tf_op jit(solution)/shard_map/pallas_call | solution.py:382
  98.3 4.8 %multiply_convert_fusion.1 = (bf16[512,1024]{1,0:T(8,128)(2,1)S(1)}, f32[512,1024]{1,0:T(8,128)}) fusion(f32[1024]{0:T(1024)S(1)} %copy-done.18, bf16[512,1024]{1,0:T(8,128)(2,1)} %get-tuple-element.89, bf16[1024,1024]{1,0:T(8,128)(2,1)} %get-tuple-element.90), kind=kOutput, calls=%fused_computation.16 | convolution fusion | flops 1076887552 | bytes 6295552 | tf_op jit(solution)/shard_map/dot_general | solution.py:649
  103.1 2.2 convolution_convert_fusion.5.refs_0_
  105.3 22.7 %shard_map.273 = (bf16[512,1024]{1,0:T(8,128)(2,1)}, bf16[512,256]{1,0:T(8,128)(2,1)}, f32[128,1024]{1,0:T(8,128)}, f32[8,1024]{1,0:T(8,128)}) custom-call(bf16[512,1024]{1,0:T(8,128)(2,1)} %convolution_convert_fusion.5.refs_0_, f32[128,1024]{1,0:T(8,128)} %get-tuple-element.92.refs_1_, bf16[128,1024]{1,0:T(8,128)(2,1)} %get-tuple-element.93.refs_2_, ...), custom_call_target="tpu_custom_call" | custom-call | bytes 30000000 | tf_op jit(solution)/shard_map/pallas_call | solution.py:382
  128.0 5.2 %fusion.41 = (f32[1024]{0:T(1024)}, bf16[512,1024]{1,0:T(8,128)(2,1)S(1)}) fusion(f32[512,1024]{1,0:T(8,128)} %get-tuple-element.151, f32[1024]{0:T(1024)S(1)} %copy-done.18, bf16[512,1024]{1,0:T(8,128)(2,1)} %get-tuple-element.95, bf16[1024,1024]{1,0:T(8,128)(2,1)} %get-tuple-element.91), kind=kOutput, calls=%fused_computation.78 | convolution fusion | flops 1080032256 | bytes 6299648 | tf_op jit(solution)/shard_map/dot_general | solution.py:661
  133.2 2.5 convolution_convert_fusion.4.refs_0_
  135.7 22.4 %shard_map.274 = (bf16[512,1024]{1,0:T(8,128)(2,1)}, f32[8,1024]{1,0:T(8,128)}) custom-call(bf16[512,1024]{1,0:T(8,128)(2,1)} %convolution_convert_fusion.4.refs_0_, f32[128,1024]{1,0:T(8,128)} %get-tuple-element.96.refs_1_, f32[128,1024]{1,0:T(8,128)} %get-tuple-element.97.refs_2_, f32[128,128]{1,0:T(8,128)} %get-tuple-element.98.refs_3_, ...), custom_call_target="tpu_custom_call" | custom-call | bytes 30000000 | tf_op jit(solution)/shard_map/pallas_call | solution.py:382
  158.0 1.7 convolution_convert_fusion.8
  159.8 3.5 %fusion.37 = (f32[4,64]{1,0:T(4,128)S(1)}, bf16[512,4,64]{0,2,1:T(8,128)(2,1)S(1)}) fusion(bf16[512,4,64]{0,2,1:T(8,128)(2,1)S(1)} %bitcast.76, f32[4,512]{1,0:T(4,128)S(1)} %log_add_fusion, f32[4,512,512]{1,2,0:T(8,128)} %copy-done, pred[512,512]{0,1:T(8,128)(4,1)S(1)} %broadcast_compare_fusion), kind=kOutput, calls=%fused_computation.76 | convolution fusion | flops 138673920 | bytes 4989952 | tf_op jit(solution)/shard_map/while/body/eval_jaxpr/hqk,qhd->khd/dot_general | solution.py:48
  163.2 2.8 fusion.43
  166.0 7.4 %fusion.21 = bf16[4,64,512]{2,1,0:T(8,128)(2,1)S(1)} fusion(bf16[512,4,64]{0,2,1:T(8,128)(2,1)S(1)} %bitcast.75, f32[4,512,512]{1,2,0:T(8,128)} %fusion.43, f32[4,512,512]{1,2,0:T(8,128)} %copy-done, f32[4,512]{1,0:T(4,128)S(1)} %log_add_fusion, pred[512,512]{0,1:T(8,128)(4,1)S(1)} %broadcast_compare_fusion), kind=kOutput, calls=%fused_computation.30 | convolution fusion | flops 145885696 | bytes 9183232 | tf_op jit(solution)/shard_map/while/body/eval_jaxpr/hqk,qhd->khd/dot_general | solution.py:55
  173.4 8.8 %fusion.36 = (f32[4,64]{1,0:T(4,128)S(1)}, bf16[512,4,64]{0,2,1:T(8,128)(2,1)S(1)}) fusion(bf16[512,4,64]{0,2,1:T(8,128)(2,1)S(1)} %bitcast.71, f32[4,512,512]{1,2,0:T(8,128)} %fusion.43, f32[4,512]{1,0:T(4,128)S(1)} %log_add_fusion, f32[4,512,512]{1,2,0:T(8,128)} %copy-done, pred[512,512]{0,1:T(8,128)(4,1)S(1)} %broadcast_compare_fusion), kind=kOutput, calls=%fused_computation.75 | convolution fusion | flops 146016512 | bytes 9184256 | tf_op jit(solution)/shard_map/while/body/eval_jaxpr/hqk,khd->qhd/dot_general | solution.py:54
  182.3 1.0 convolution_convert_fusion.2
  184.1 1.8 collective-permute-start
  187.8 1.3 convolution_convert_fusion.1
  190.7 1.3 convolution_convert_fusion
  192.9 1.8 collective-permute-start.12
  194.7 2.0 convolution_convert_fusion.3.refs_0_
  198.2 29.7 %shard_map.275 = (f32[512,256]{1,0:T(8,128)}, f32[24,256]{1,0:T(8,128)}) custom-call(bf16[512,1024]{1,0:T(8,128)(2,1)} %convolution_convert_fusion.3.refs_0_, bf16[512,1024]{1,0:T(8,128)(2,1)} %get-tuple-element.99.refs_1_, f32[8,1024]{1,0:T(8,128)} %get-tuple-element.100.refs_2_, f32[8,1024]{1,0:T(8,128)} %get-tuple-element.101.refs_3_, ...), custom_call_target="tpu_custom_call" | custom-call | bytes 30000000 | tf_op jit(solution)/shard_map/pallas_call | solution.py:474
  227.9 1.4 fusion.38
  230.6 0.9 add_convert_fusion.11
  231.5 1.1 collective-permute-start.5
  232.6 1.1 add_convert_fusion.8
  234.6 1.4 add_convert_fusion.5
  236.0 1.8 collective-permute-start.9
  237.8 1.9 collective-permute-done.5
  240.6 7.5 %collective-permute-done.1 = bf16[256,768]{0,1:T(8,128)(2,1)S(1)} collective-permute-done((bf16[256,768]{0,1:T(8,128)(2,1)S(1)}, bf16[256,768]{0,1:T(8,128)(2,1)S(1)}, u32[]{:S(2)}, u32[]{:S(2)}) %collective-permute-start.1) | collective-permute-done | bytes 393248 | tf_op jit(solution)/shard_map/ppermute | solution.py:569
  248.3 11.0 %collective-permute-done.9 = bf16[256,1024]{1,0:T(8,128)(2,1)S(1)} collective-permute-done((bf16[256,1024]{1,0:T(8,128)(2,1)S(1)}, bf16[256,1024]{1,0:T(8,128)(2,1)S(1)}, u32[]{:S(2)}, u32[]{:S(2)}) %collective-permute-start.9) | collective-permute-done | bytes 524320 | tf_op jit(solution)/shard_map/ppermute | solution.py:569
  259.6 2.5 collective-permute-done.6
  262.2 1.6 collective-permute-start.7
  263.8 9.6 %collective-permute-done.13 = bf16[1024,256]{1,0:T(8,128)(2,1)S(1)} collective-permute-done((bf16[1024,256]{1,0:T(8,128)(2,1)S(1)}, bf16[1024,256]{1,0:T(8,128)(2,1)S(1)}, u32[]{:S(2)}, u32[]{:S(2)}) %collective-permute-start.13) | collective-permute-done | bytes 524320 | tf_op jit(solution)/shard_map/ppermute | solution.py:569
  273.6 8.2 %collective-permute-done.2 = bf16[256,768]{0,1:T(8,128)(2,1)S(1)} collective-permute-done((bf16[256,768]{0,1:T(8,128)(2,1)S(1)}, bf16[256,768]{0,1:T(8,128)(2,1)S(1)}, u32[]{:S(2)}, u32[]{:S(2)}) %collective-permute-start.2) | collective-permute-done | bytes 393248 | tf_op jit(solution)/shard_map/ppermute | solution.py:569
  281.9 1.6 collective-permute-start.3
  283.5 9.6 %collective-permute-done.10 = bf16[256,1024]{1,0:T(8,128)(2,1)S(1)} collective-permute-done((bf16[256,1024]{1,0:T(8,128)(2,1)S(1)}, bf16[256,1024]{1,0:T(8,128)(2,1)S(1)}, u32[]{:S(2)}, u32[]{:S(2)}) %collective-permute-start.10) | collective-permute-done | bytes 524320 | tf_op jit(solution)/shard_map/ppermute | solution.py:569
  293.3 1.6 collective-permute-start.11
  295.5 7.9 %collective-permute-done.14 = bf16[1024,256]{1,0:T(8,128)(2,1)S(1)} collective-permute-done((bf16[1024,256]{1,0:T(8,128)(2,1)S(1)}, bf16[1024,256]{1,0:T(8,128)(2,1)S(1)}, u32[]{:S(2)}, u32[]{:S(2)}) %collective-permute-start.14) | collective-permute-done | bytes 524320 | tf_op jit(solution)/shard_map/ppermute | solution.py:569
  303.6 1.6 collective-permute-start.15
  305.3 1.1 copy.52
  306.4 2.3 convert_add_fusion.1
  308.7 8.1 %collective-permute-done.15 = bf16[1024,256]{1,0:T(8,128)(2,1)S(1)} collective-permute-done((bf16[1024,256]{1,0:T(8,128)(2,1)S(1)}, bf16[1024,256]{1,0:T(8,128)(2,1)S(1)}, u32[]{:S(2)}, u32[]{:S(2)}) %collective-permute-start.15) | collective-permute-done | bytes 524320 | tf_op jit(solution)/shard_map/ppermute | solution.py:579
  316.8 1.1 convert_add_fusion
  (107 shorter events, 17.2 us)
Async XLA Ops:
  57.7 2.8 copy-start.11
  57.7 2.8 copy-start.12
  60.4 0.7 copy-start.10
  62.5 2.0 copy-start
  64.5 1.3 copy-start.7
  65.7 32.5 %copy-start.18 = (f32[1024]{0:T(1024)S(1)}, f32[1024]{0:T(1024)}, u32[]{:S(2)}) copy-start(f32[1024]{0:T(1024)} %param.26) | copy-start | bytes 12292
  98.2 4.8 %copy-start.14 = (bf16[1024,1024]{1,0:T(8,128)(2,1)S(1)}, bf16[1024,1024]{1,0:T(8,128)(2,1)}, u32[]{:S(2)}) copy-start(bf16[1024,1024]{1,0:T(8,128)(2,1)} %get-tuple-element.91) | copy-start | bytes 6291460
  103.1 2.2 copy-start.25
  128.0 5.2 %copy-start.13 = (bf16[1024,1024]{1,0:T(8,128)(2,1)S(1)}, bf16[1024,1024]{1,0:T(8,128)(2,1)}, u32[]{:S(2)}) copy-start(bf16[1024,1024]{1,0:T(8,128)(2,1)} %get-tuple-element.90) | copy-start | bytes 6291460
  133.2 2.5 copy-start.27
  163.2 19.0 %copy-start.19 = (bf16[512,4,64]{0,2,1:T(8,128)(2,1)}, bf16[512,4,64]{0,2,1:T(8,128)(2,1)S(1)}, u32[]{:S(2)}) copy-start(bf16[512,4,64]{0,2,1:T(8,128)(2,1)S(1)} %get-tuple-element.139) | copy-start | bytes 786436
  173.4 8.9 %copy-start.21 = (bf16[4,64,512]{2,1,0:T(8,128)(2,1)}, bf16[4,64,512]{2,1,0:T(8,128)(2,1)S(1)}, u32[]{:S(2)}) copy-start(bf16[4,64,512]{2,1,0:T(8,128)(2,1)S(1)} %fusion.21) | copy-start | bytes 786436
  173.4 8.9 %copy-start.6 = (bf16[512,1024]{1,0:T(8,128)(2,1)S(1)}, bf16[512,1024]{1,0:T(8,128)(2,1)}, u32[]{:S(2)}) copy-start(bf16[512,1024]{1,0:T(8,128)(2,1)} %get-tuple-element.85.refs_1_) | copy-start | bytes 3145732
  182.2 1.0 copy-start.23
  182.3 3.7 %copy-start.1 = (bf16[512,1024]{1,0:T(8,128)(2,1)S(1)}, bf16[512,1024]{1,0:T(8,128)(2,1)}, u32[]{:S(2)}) copy-start(bf16[512,1024]{1,0:T(8,128)(2,1)} %get-tuple-element.99.refs_1_) | copy-start | bytes 3145732
  183.3 3.8 %copy-start.4 = (bf16[1024,768]{0,1:T(8,128)(2,1)}, bf16[1024,768]{0,1:T(8,128)(2,1)S(1)}, u32[]{:S(2)}) copy-start(bf16[1024,768]{0,1:T(8,128)(2,1)S(1)} %convolution_convert_fusion.2) | copy-start | bytes 4718596
  183.3 4.5 %copy-start.17 = (bf16[512,1024]{1,0:T(8,128)(2,1)S(1)}, bf16[512,1024]{1,0:T(8,128)(2,1)}, u32[]{:S(2)}) copy-start(bf16[512,1024]{1,0:T(8,128)(2,1)} %get-tuple-element.89) | copy-start | bytes 3145732
  183.3 4.5 %copy-start.28 = (bf16[512,1024]{1,0:T(8,128)(2,1)S(1)}, bf16[512,1024]{1,0:T(8,128)(2,1)}, u32[]{:S(2)}) copy-start(bf16[512,1024]{1,0:T(8,128)(2,1)} %copy-done.27) | copy-start | bytes 3145732
  184.1 48.5 %collective-permute-start = (bf16[256,768]{0,1:T(8,128)(2,1)}, bf16[256,768]{0,1:T(8,128)(2,1)S(1)}, u32[]{:S(2)}, u32[]{:S(2)}) collective-permute-start(bf16[256,768]{0,1:T(8,128)(2,1)} %constant_dynamic-slice_fusion.3), channel_id=1, source_target_pairs={{0,4},{4,8},{8,12},{12,0},{1,5},{5,9},{9,13},{13,1},{2,6},{6,10},{... | collective-permute-start | bytes 1179656 | tf_op jit(solution)/shard_map/ppermute | solution.py:569
  187.1 3.6 %copy-start.16 = (bf16[512,1024]{1,0:T(8,128)(2,1)S(1)}, bf16[512,1024]{1,0:T(8,128)(2,1)}, u32[]{:S(2)}) copy-start(bf16[512,1024]{1,0:T(8,128)(2,1)} %get-tuple-element.95) | copy-start | bytes 3145732
  187.1 3.6 %copy-start.26 = (bf16[512,1024]{1,0:T(8,128)(2,1)S(1)}, bf16[512,1024]{1,0:T(8,128)(2,1)}, u32[]{:S(2)}) copy-start(bf16[512,1024]{1,0:T(8,128)(2,1)} %copy-done.25) | copy-start | bytes 3145732
  187.1 43.5 %collective-permute-start.4 = (bf16[256,256]{1,0:T(8,128)(2,1)}, bf16[256,256]{1,0:T(8,128)(2,1)}, u32[]{:S(2)}, u32[]{:S(2)}) collective-permute-start(bf16[256,256]{1,0:T(8,128)(2,1)} %constant_dynamic-slice_fusion.2), channel_id=1, source_target_pairs={{0,4},{4,8},{8,12},{12,0},{1,5},{5,9},{9,13},{13,1},{2,6},{6,10},{... | collective-permute-start | bytes 393224 | tf_op jit(solution)/shard_map/ppermute | solution.py:569
  189.1 2.9 copy-start.2
  190.1 4.7 %copy-start.15 = (bf16[1024,768]{1,0:T(8,128)(2,1)S(1)}, bf16[1024,768]{1,0:T(8,128)(2,1)}, u32[]{:S(2)}) copy-start(bf16[1024,768]{1,0:T(8,128)(2,1)} %get-tuple-element.86) | copy-start | bytes 4718596
  190.1 4.7 %copy-start.20 = (bf16[512,4,64]{0,2,1:T(8,128)(2,1)S(1)}, bf16[512,4,64]{0,2,1:T(8,128)(2,1)}, u32[]{:S(2)}) copy-start(bf16[512,4,64]{0,2,1:T(8,128)(2,1)} %copy-done.19) | copy-start | bytes 786436
  190.1 4.7 %copy-start.22 = (bf16[4,64,512]{2,1,0:T(8,128)(2,1)S(1)}, bf16[4,64,512]{2,1,0:T(8,128)(2,1)}, u32[]{:S(2)}) copy-start(bf16[4,64,512]{2,1,0:T(8,128)(2,1)} %copy-done.21) | copy-start | bytes 786436
  190.1 4.7 %copy-start.24 = (bf16[512,4,64]{0,2,1:T(8,128)(2,1)S(1)}, bf16[512,4,64]{0,2,1:T(8,128)(2,1)}, u32[]{:S(2)}) copy-start(bf16[512,4,64]{0,2,1:T(8,128)(2,1)} %copy-done.23) | copy-start | bytes 786436
  190.1 44.6 %collective-permute-start.8 = (bf16[256,1024]{1,0:T(8,128)(2,1)}, bf16[256,1024]{1,0:T(8,128)(2,1)}, u32[]{:S(2)}, u32[]{:S(2)}) collective-permute-start(bf16[256,1024]{1,0:T(8,128)(2,1)} %constant_dynamic-slice_fusion.1), channel_id=1, source_target_pairs={{0,4},{4,8},{8,12},{12,0},{1,5},{5,9},{9,13},{13,1},{2,6},{6,10},{... | collective-permute-start | bytes 1572872 | tf_op jit(solution)/shard_map/ppermute | solution.py:569
  192.9 46.9 %collective-permute-start.12 = (bf16[1024,256]{1,0:T(8,128)(2,1)}, bf16[1024,256]{1,0:T(8,128)(2,1)S(1)}, u32[]{:S(2)}, u32[]{:S(2)}) collective-permute-start(bf16[1024,256]{1,0:T(8,128)(2,1)} %constant_dynamic-slice_fusion), channel_id=1, source_target_pairs={{0,4},{4,8},{8,12},{12,0},{1,5},{5,9},{9,13},{13,1},{2,6},{6,10},{... | collective-permute-start | bytes 1572872 | tf_op jit(solution)/shard_map/ppermute | solution.py:569
  231.5 16.6 %copy-start.5 = (bf16[1024,768]{0,1:T(8,128)(2,1)S(1)}, bf16[1024,768]{0,1:T(8,128)(2,1)}, u32[]{:S(2)}) copy-start(bf16[1024,768]{0,1:T(8,128)(2,1)} %copy-done.4) | copy-start | bytes 4718596
  231.5 8.2 %collective-permute-start.5 = (bf16[256,256]{1,0:T(8,128)(2,1)S(1)}, bf16[256,256]{1,0:T(8,128)(2,1)S(1)}, u32[]{:S(2)}, u32[]{:S(2)}) collective-permute-start(bf16[256,256]{1,0:T(8,128)(2,1)S(1)} %add_convert_fusion.11), channel_id=1, source_target_pairs={{0,4},{4,8},{8,12},{12,0},{1,5},{5,9},{9,13},{13,1},{2,6},{6,10},{... | collective-permute-start | bytes 393224 | tf_op jit(solution)/shard_map/ppermute | solution.py:569
  233.7 25.6 %copy-start.3 = (bf16[1024,1024]{1,0:T(8,128)(2,1)S(1)}, bf16[1024,1024]{1,0:T(8,128)(2,1)}, u32[]{:S(2)}) copy-start(bf16[1024,1024]{1,0:T(8,128)(2,1)} %copy-done.2) | copy-start | bytes 6291460
  233.8 14.4 %collective-permute-start.1 = (bf16[256,768]{0,1:T(8,128)(2,1)S(1)}, bf16[256,768]{0,1:T(8,128)(2,1)S(1)}, u32[]{:S(2)}, u32[]{:S(2)}) collective-permute-start(bf16[256,768]{0,1:T(8,128)(2,1)S(1)} %add_convert_fusion.8), channel_id=1, source_target_pairs={{0,4},{4,8},{8,12},{12,0},{1,5},{5,9},{9,13},{13,1},{2,6},{6,10},{... | collective-permute-start | bytes 1179656 | tf_op jit(solution)/shard_map/ppermute | solution.py:569
  236.0 23.3 %collective-permute-start.9 = (bf16[256,1024]{1,0:T(8,128)(2,1)S(1)}, bf16[256,1024]{1,0:T(8,128)(2,1)S(1)}, u32[]{:S(2)}, u32[]{:S(2)}) collective-permute-start(bf16[256,1024]{1,0:T(8,128)(2,1)S(1)} %add_convert_fusion.5), channel_id=1, source_target_pairs={{0,4},{4,8},{8,12},{12,0},{1,5},{5,9},{9,13},{13,1},{2,6},{6,10},{... | collective-permute-start | bytes 1572872 | tf_op jit(solution)/shard_map/ppermute | solution.py:569
  239.7 22.4 %collective-permute-start.6 = (bf16[256,256]{1,0:T(8,128)(2,1)S(1)}, bf16[256,256]{1,0:T(8,128)(2,1)S(1)}, u32[]{:S(2)}, u32[]{:S(2)}) collective-permute-start(bf16[256,256]{1,0:T(8,128)(2,1)S(1)} %add_convert_fusion.10), channel_id=1, source_target_pairs={{0,4},{4,8},{8,12},{12,0},{1,5},{5,9},{9,13},{13,1},{2,6},{6,10},{... | collective-permute-start | bytes 393224 | tf_op jit(solution)/shard_map/ppermute | solution.py:569
  240.0 33.4 %collective-permute-start.13 = (bf16[1024,256]{1,0:T(8,128)(2,1)S(1)}, bf16[1024,256]{1,0:T(8,128)(2,1)S(1)}, u32[]{:S(2)}, u32[]{:S(2)}) collective-permute-start(bf16[1024,256]{1,0:T(8,128)(2,1)S(1)} %add_convert_fusion.2), channel_id=1, source_target_pairs={{0,4},{4,8},{8,12},{12,0},{1,5},{5,9},{9,13},{13,1},{2,6},{6,10},{... | collective-permute-start | bytes 1572872 | tf_op jit(solution)/shard_map/ppermute | solution.py:569
  248.2 33.6 %collective-permute-start.2 = (bf16[256,768]{0,1:T(8,128)(2,1)S(1)}, bf16[256,768]{0,1:T(8,128)(2,1)S(1)}, u32[]{:S(2)}, u32[]{:S(2)}) collective-permute-start(bf16[256,768]{0,1:T(8,128)(2,1)S(1)} %add_convert_fusion.7), channel_id=1, source_target_pairs={{0,4},{4,8},{8,12},{12,0},{1,5},{5,9},{9,13},{13,1},{2,6},{6,10},{... | collective-permute-start | bytes 1179656 | tf_op jit(solution)/shard_map/ppermute | solution.py:569
  259.6 33.5 %collective-permute-start.10 = (bf16[256,1024]{1,0:T(8,128)(2,1)S(1)}, bf16[256,1024]{1,0:T(8,128)(2,1)S(1)}, u32[]{:S(2)}, u32[]{:S(2)}) collective-permute-start(bf16[256,1024]{1,0:T(8,128)(2,1)S(1)} %add_convert_fusion.4), channel_id=1, source_target_pairs={{0,4},{4,8},{8,12},{12,0},{1,5},{5,9},{9,13},{13,1},{2,6},{6,10},{... | collective-permute-start | bytes 1572872 | tf_op jit(solution)/shard_map/ppermute | solution.py:569
  262.2 32.6 %collective-permute-start.7 = (bf16[256,256]{1,0:T(8,128)(2,1)S(1)}, bf16[256,256]{1,0:T(8,128)(2,1)S(1)}, u32[]{:S(2)}, u32[]{:S(2)}) collective-permute-start(bf16[256,256]{1,0:T(8,128)(2,1)S(1)} %add_convert_fusion.9), channel_id=1, source_target_pairs={{0,16},{16,0},{1,17},{17,1},{2,18},{18,2},{3,19},{19,3},{4,20},{20... | collective-permute-start | bytes 393224 | tf_op jit(solution)/shard_map/ppermute | solution.py:579
  273.6 29.9 %collective-permute-start.14 = (bf16[1024,256]{1,0:T(8,128)(2,1)S(1)}, bf16[1024,256]{1,0:T(8,128)(2,1)S(1)}, u32[]{:S(2)}, u32[]{:S(2)}) collective-permute-start(bf16[1024,256]{1,0:T(8,128)(2,1)S(1)} %add_convert_fusion.1), channel_id=1, source_target_pairs={{0,4},{4,8},{8,12},{12,0},{1,5},{5,9},{9,13},{13,1},{2,6},{6,10},{... | collective-permute-start | bytes 1572872 | tf_op jit(solution)/shard_map/ppermute | solution.py:569
  281.9 23.2 %collective-permute-start.3 = (bf16[256,768]{0,1:T(8,128)(2,1)S(1)}, bf16[256,768]{0,1:T(8,128)(2,1)S(1)}, u32[]{:S(2)}, u32[]{:S(2)}) collective-permute-start(bf16[256,768]{0,1:T(8,128)(2,1)S(1)} %add_convert_fusion.6), channel_id=1, source_target_pairs={{0,16},{16,0},{1,17},{17,1},{2,18},{18,2},{3,19},{19,3},{4,20},{20... | collective-permute-start | bytes 1179656 | tf_op jit(solution)/shard_map/ppermute | solution.py:579
  293.3 13.2 %collective-permute-start.11 = (bf16[256,1024]{1,0:T(8,128)(2,1)S(1)}, bf16[256,1024]{1,0:T(8,128)(2,1)}, u32[]{:S(2)}, u32[]{:S(2)}) collective-permute-start(bf16[256,1024]{1,0:T(8,128)(2,1)S(1)} %add_convert_fusion.3), channel_id=1, source_target_pairs={{0,16},{16,0},{1,17},{17,1},{2,18},{18,2},{3,19},{19,3},{4,20},{20... | collective-permute-start | bytes 1572872 | tf_op jit(solution)/shard_map/ppermute | solution.py:579
  303.6 13.2 %collective-permute-start.15 = (bf16[1024,256]{1,0:T(8,128)(2,1)S(1)}, bf16[1024,256]{1,0:T(8,128)(2,1)S(1)}, u32[]{:S(2)}, u32[]{:S(2)}) collective-permute-start(bf16[1024,256]{1,0:T(8,128)(2,1)S(1)} %add_convert_fusion), channel_id=1, source_target_pairs={{0,16},{16,0},{1,17},{17,1},{2,18},{18,2},{3,19},{19,3},{4,20},{20... | collective-permute-start | bytes 1572872 | tf_op jit(solution)/shard_map/ppermute | solution.py:579
  306.4 11.5 %copy-start.9 = (bf16[512,256]{1,0:T(8,128)(2,1)S(1)}, bf16[512,256]{1,0:T(8,128)(2,1)}, u32[]{:S(2)}) copy-start(bf16[512,256]{1,0:T(8,128)(2,1)} %get-tuple-element.173) | copy-start | bytes 786436
  306.4 12.2 %copy-start.8 = (f32[512,256]{1,0:T(8,128)S(1)}, f32[512,256]{1,0:T(8,128)}, u32[]{:S(2)}) copy-start(f32[512,256]{1,0:T(8,128)} %get-tuple-element.174) | copy-start | bytes 1572868
